TPU v7x, 32 devices: a whole 2x2x4 slice. The times are simulated.
32 devices in a mesh: slab: 2 (over y), gz: 16 (over z, x, core).
Axes of the slice: x: 2, y: 2, z: 4, core: 2. Of those that a mesh axis runs over, the one named last changes fastest.
Arguments:
- eigvecs: bfloat16 [32, 2, 3, 256, 576], P(('slab', 'gz')), parts along dimension 0, may hold values from -6 to 6
- gauge_links: bfloat16 [32, 3, 2, 3, 3, 576], P(('slab', 'gz')), parts along dimension 0, may hold values from -3.5 to 3.5
- momenta: int32 [8, 3], replicated, may hold values from -2 to 2
- directions: int32 [8], replicated, may hold values from 0 to 2, as said below
Outputs:
- elementals: float32 [16, 2, 256, 256], P('slab', None, 'gz'), parts along dimension 0
There are 2 independent parts, one for each index of `slab`. A program takes and returns all parts, laid end to end along the dimension named above; an argument that names none is the same for every part. Nothing has to cross between parts.
Inputs may be any that keep to these rules, and one draw needn't show every extreme that they name: Each of the three directions is named by at least one momentum.
All inputs are finite; a program needn't handle non-finite values.
Results may differ from a plain program's by a relative error of at most 0.0045.
Values may be sent and summed in bfloat16 or wider, within the bound.
No kernel may reach another device: no remote copies, remote signals or barrier semaphores. Data moves between devices by JAX's collectives and lax.ppermute only.
A program may use at most 64 MiB of HBM per device.

v0:
```python
import math

import jax
import jax.numpy as jnp
from jax import lax
from jax.sharding import PartitionSpec as P

NX = 96
NY = 96
ZEXT = 96


two_pi = 2.0 * math.pi


def shifted(block, axis, distance):
    devices = range(lax.axis_size(axis))
    route = [((i - distance) % len(devices), i) for i in devices]
    return lax.ppermute(block, axis, route)


def apply_link(gauge_link, vectors, adjoint):
    real_rows = []
    imag_rows = []
    for i in range(3):
        sum_real = 0.0
        sum_imag = 0.0
        for j in range(3):
            if adjoint:
                link_real = gauge_link[0, j, i, :]
                link_imag = -gauge_link[1, j, i, :]
            else:
                link_real = gauge_link[0, i, j, :]
                link_imag = gauge_link[1, i, j, :]
            link_real = link_real.astype(jnp.float32)[None, :]
            link_imag = link_imag.astype(jnp.float32)[None, :]
            vec_real = vectors[0, j]
            vec_imag = vectors[1, j]
            sum_real = sum_real + link_real * vec_real - link_imag * vec_imag
            sum_imag = sum_imag + link_real * vec_imag + link_imag * vec_real
        real_rows.append(sum_real)
        imag_rows.append(sum_imag)
    return jnp.stack([jnp.stack(real_rows), jnp.stack(imag_rows)])


def from_side(face, stride, sign, at_edge, wrap_inside):
    near = shifted(face, "gz", -sign * stride)
    if wrap_inside:
        far = shifted(face, "gz", 3 * sign * stride)
        return jnp.where(at_edge, far, near)
    return near


def body(eigvecs, gauge_links, momenta, directions):
    device_count = lax.axis_size("gz")
    my_index = lax.axis_index("gz")
    vectors = eigvecs[0]
    links = gauge_links[0]
    side_x = NX // 4
    side_y = NY // 4
    site_count = vectors.shape[-1]
    depth = site_count // (side_x * side_y)
    vector_count = vectors.shape[2]
    z_extent = depth * (device_count // 16)
    factor = (3.0 * NX * NY * z_extent) ** (-0.5)
    block_x = my_index // 4 % 4
    block_y = my_index % 4
    block_z = my_index // 16
    coords = (block_x, block_y, block_z)
    strides = (4, 1, 16)
    axis_of = (4, 5, 3)
    grid_shape = (2, 3, vector_count, depth, side_x, side_y)
    grid_v = vectors.reshape(grid_shape)
    displaced = []
    for d in range(3):
        link = links[d]
        backward = apply_link(link, vectors, True).astype(jnp.bfloat16)
        grid_b = backward.reshape(grid_shape)
        axis = axis_of[d]
        length = grid_v.shape[axis]
        low_face = lax.slice_in_dim(grid_v, 0, 1, 1, axis)
        high_face = lax.slice_in_dim(grid_b, length - 1, length, 1, axis)
        upper = from_side(low_face, strides[d], 1, coords[d] == 3, d < 2)
        lower = from_side(high_face, strides[d], -1, coords[d] == 0, d < 2)
        ahead = jnp.concatenate(
            [lax.slice_in_dim(grid_v, 1, length, 1, axis), upper], axis
        ).reshape(vectors.shape)
        behind = jnp.concatenate(
            [lower, lax.slice_in_dim(grid_b, 0, length - 1, 1, axis)], axis
        ).reshape(vectors.shape)
        forward = apply_link(link, ahead, False)
        displaced.append((0.5 * (forward - behind.astype(jnp.float32))).astype(jnp.bfloat16))
    right_sides = jnp.stack(
        [
            jnp.stack([jnp.stack([disp[0], -disp[1]]), jnp.stack([disp[1], disp[0]])])
            for disp in displaced
        ]
    )
    site_index = jnp.arange(site_count)
    global_x = block_x * side_x + site_index // side_y % side_x
    global_y = block_y * side_y + site_index % side_y
    global_z = block_z * depth + site_index // (side_x * side_y)
    blocks = []
    for p in range(momenta.shape[0]):
        x_mod = jnp.mod(momenta[p, 0] * global_x, NX).astype(jnp.float32)
        y_mod = jnp.mod(momenta[p, 1] * global_y, NY).astype(jnp.float32)
        z_mod = jnp.mod(momenta[p, 2] * global_z, ZEXT).astype(jnp.float32)
        phase_angle = two_pi * (x_mod / NX + y_mod / NY + z_mod / ZEXT)
        cos_part = jnp.cos(phase_angle)[None, None, :]
        sin_part = jnp.sin(phase_angle)[None, None, :]
        left_real = vectors[0] * cos_part + vectors[1] * sin_part
        left_imag = vectors[0] * sin_part - vectors[1] * cos_part
        left_side = jnp.stack([left_real, left_imag]).astype(jnp.bfloat16)
        right_side = lax.dynamic_index_in_dim(right_sides, directions[p], 0, keepdims=False)
        blocks.append(
            lax.dot_general(
                left_side,
                right_side,
                (((0, 1, 3), (1, 2, 4)), ((), ())),
                preferred_element_type=jnp.float32,
            )
        )
    owned = lax.psum_scatter(jnp.stack(blocks, 1) * factor, "gz", scatter_dimension=0, tiled=True)
    return jnp.transpose(owned, (1, 2, 0, 3))


def solution(mesh):
    return jax.shard_map(
        body,
        mesh=mesh,
        in_specs=(
            P(("slab", "gz"), None, None, None, None),
            P(("slab", "gz"), None, None, None, None, None),
            P(),
            P(),
        ),
        out_specs=P("slab", None, "gz", None),
        check_vma=False,
    )
```

profile of v0, /device:TPU:0, one launch (start us, length us, event | category | flops | bytes accessed | tf_op | source)
XLA Modules:
  0.0 239.5 jit_solution(10187513158071683551)
XLA Ops:
  6.5 1.8 slice.731
  8.3 5.4 %collective-permute-start.3 = (bf16[2,3,256,1,24,1]{2,5,4,1,0,3:T(2,128)(2,1)}, bf16[2,3,256,1,24,1]{2,5,4,1,0,3:T(2,128)(2,1)}, u32[]{:S(2)}, u32[]{:S(2)}) collective-permute-start(bf16[2,3,256,1,24,1]{2,5,4,1,0,3:T(2,128)(2,1)} %slice.731), channel_id=1, source_target_pairs={{1,0},{2,1},{3,2},{4,3},{5,4},{6,5},{7,6},{8,7},{9,8},{10,9},{11,1... | collective-permute-start | bytes 221192 | tf_op jit(solution)/shard_map/ppermute | solution.py:19
  13.8 1.4 slice_bitcast_fusion.20
  26.6 1.5 fusion.511
  29.7 2.2 fusion.285
  32.9 3.6 %collective-permute-start.4 = (bf16[2,3,256,1,24,1]{2,5,4,3,1,0:T(2,128)(2,1)}, bf16[2,3,256,1,24,1]{2,5,4,3,1,0:T(2,128)(2,1)}, u32[]{:S(2)}, u32[]{:S(2)}) collective-permute-start(bf16[2,3,256,1,24,1]{2,5,4,3,1,0:T(2,128)(2,1)} %maximum_maximum_fusion.1), channel_id=1, source_target_pairs={{3,0},{4,1},{5,2},{6,3},{7,4},{8,5},{9,6},{10,7},{11,8},{12,9},{13... | collective-permute-start | bytes 221192 | tf_op jit(solution)/shard_map/ppermute | solution.py:19
  49.5 1.4 fusion.460
  50.9 1.6 convert_reduce_fusion.8
  53.8 2.2 slice.730
  70.3 1.4 reshape.8046
  101.1 2.0 fusion.501
  103.1 1.9 fusion.479
  104.9 1.8 fusion.481
  106.7 2.0 fusion.483
  108.7 2.0 fusion.485
  110.7 1.9 fusion.487
  112.6 1.8 fusion.489
  114.4 2.0 fusion.491
  120.2 1.5 fusion.59
  121.9 1.5 fusion.55
  125.0 1.9 collective-permute-start.1
  147.2 1.9 pad_maximum_fusion
  158.3 2.3 broadcast_multiply_fusion
  160.6 72.1 %reduce-scatter.2.cloned.1.call-done = f32[16,8,2,256]{3,0,2,1:T(8,128)} async-done(((f32[256,8,2,256]{3,0,2,1:T(8,128)}), f32[16,8,2,256]{3,0,2,1:T(8,128)}) %reduce-scatter.2.cloned.1.call-update) | async-done | bytes 262160 | tf_op jit(solution)/shard_map/reduce_scatter | solution.py:123
  (369 shorter events, 89.8 us)
Async XLA Ops:
  6.5 226.1 %reduce-scatter.2.cloned.1.call-start = ((), (), s32[]{:S(2)}) async-start(), calls=%async_computation.1 | async-start | bytes 4456448 | tf_op jit(solution)/shard_map/reduce_scatter | solution.py:123
  8.3 124.4 %collective-permute-start.3 = (bf16[2,3,256,1,24,1]{2,5,4,1,0,3:T(2,128)(2,1)}, bf16[2,3,256,1,24,1]{2,5,4,1,0,3:T(2,128)(2,1)}, u32[]{:S(2)}, u32[]{:S(2)}) collective-permute-start(bf16[2,3,256,1,24,1]{2,5,4,1,0,3:T(2,128)(2,1)} %slice.731), channel_id=1, source_target_pairs={{1,0},{2,1},{3,2},{4,3},{5,4},{6,5},{7,6},{8,7},{9,8},{10,9},{11,1... | collective-permute-start | bytes 221192 | tf_op jit(solution)/shard_map/ppermute | solution.py:19
  13.8 119.1 %collective-permute-start.2 = (bf16[2,3,256,1,24,1]{2,5,4,1,0,3:T(2,128)(2,1)}, bf16[2,3,256,1,24,1]{2,5,4,1,0,3:T(2,128)(2,1)}, u32[]{:S(2)}, u32[]{:S(2)}) collective-permute-start(bf16[2,3,256,1,24,1]{2,5,4,1,0,3:T(2,128)(2,1)} %slice.731), channel_id=1, source_target_pairs={{13,0},{14,1},{15,2},{0,3},{1,4},{2,5},{3,6},{4,7},{5,8},{6,9},{7,... | collective-permute-start | bytes 221192 | tf_op jit(solution)/shard_map/ppermute | solution.py:19
  15.8 6.4 %copy-start.78 = (f32[576]{0:T(1024)}, f32[576]{0:T(1024)S(1)}, u32[]{:S(2)}) copy-start(f32[576]{0:T(1024)S(1)} %get-tuple-element.51) | copy-start | bytes 6916
  15.8 6.4 %copy-start.80 = (f32[576]{0:T(1024)}, f32[576]{0:T(1024)S(1)}, u32[]{:S(2)}) copy-start(f32[576]{0:T(1024)S(1)} %get-tuple-element.55) | copy-start | bytes 6916
  15.8 7.2 %copy-start.82 = (f32[576]{0:T(1024)}, f32[576]{0:T(1024)S(1)}, u32[]{:S(2)}) copy-start(f32[576]{0:T(1024)S(1)} %get-tuple-element.57) | copy-start | bytes 6916
  15.8 7.3 %copy-start.84 = (f32[576]{0:T(1024)}, f32[576]{0:T(1024)S(1)}, u32[]{:S(2)}) copy-start(f32[576]{0:T(1024)S(1)} %get-tuple-element.53) | copy-start | bytes 6916
  16.6 5.7 %copy-start.60 = (f32[576]{0:T(1024)}, f32[576]{0:T(1024)S(1)}, u32[]{:S(2)}) copy-start(f32[576]{0:T(1024)S(1)} %get-tuple-element.42) | copy-start | bytes 6916
  16.6 6.4 %copy-start.62 = (f32[576]{0:T(1024)}, f32[576]{0:T(1024)S(1)}, u32[]{:S(2)}) copy-start(f32[576]{0:T(1024)S(1)} %get-tuple-element.44) | copy-start | bytes 6916
  16.6 6.4 %copy-start.64 = (f32[576]{0:T(1024)}, f32[576]{0:T(1024)S(1)}, u32[]{:S(2)}) copy-start(f32[576]{0:T(1024)S(1)} %get-tuple-element.46) | copy-start | bytes 6916
  16.6 11.6 %copy-start.58 = (f32[576]{0:T(1024)}, f32[576]{0:T(1024)S(1)}, u32[]{:S(2)}) copy-start(f32[576]{0:T(1024)S(1)} %get-tuple-element.50) | copy-start | bytes 6916
  17.2 5.9 %copy-start.87 = (f32[576]{0:T(1024)}, f32[576]{0:T(1024)S(1)}, u32[]{:S(2)}) copy-start(f32[576]{0:T(1024)S(1)} %get-tuple-element.28) | copy-start | bytes 6916
  17.9 10.2 %copy-start.66 = (f32[576]{0:T(1024)}, f32[576]{0:T(1024)S(1)}, u32[]{:S(2)}) copy-start(f32[576]{0:T(1024)S(1)} %get-tuple-element.21) | copy-start | bytes 6916
  17.9 10.2 %copy-start.69 = (f32[576]{0:T(1024)}, f32[576]{0:T(1024)S(1)}, u32[]{:S(2)}) copy-start(f32[576]{0:T(1024)S(1)} %get-tuple-element.15) | copy-start | bytes 6916
  29.7 6.8 %copy-start = (bf16[1,2,3,256,576]{3,4,2,1,0:T(8,128)(2,1)S(1)}, bf16[1,2,3,256,576]{3,4,2,1,0:T(8,128)(2,1)}, u32[]{:S(2)}) copy-start(bf16[1,2,3,256,576]{3,4,2,1,0:T(8,128)(2,1)} %param.4) | copy-start | bytes 5308420
  31.9 4.6 %copy-start.15 = (bf16[1,1,256,1,24,24]{2,5,4,3,1,0:T(8,128)(2,1)}, bf16[1,1,256,1,24,24]{2,5,4,3,1,0:T(8,128)(2,1)S(1)}, u32[]{:S(2)}) copy-start(bf16[1,1,256,1,24,24]{2,5,4,3,1,0:T(8,128)(2,1)S(1)} %get-tuple-element.154) | copy-start | bytes 884740
  31.9 5.5 %copy-start.95 = (s32[8]{0:T(128)S(1)}, s32[8]{0:T(128)}, u32[]{:S(2)}) copy-start(s32[8]{0:T(128)} %param.7) | copy-start | bytes 100
  31.9 16.2 %copy-start.17 = (s32[8,3]{0,1:T(4,128)S(1)}, s32[8,3]{0,1:T(4,128)}, u32[]{:S(2)}) copy-start(s32[8,3]{0,1:T(4,128)} %param.6) | copy-start | bytes 292
  32.8 105.4 %collective-permute-start.5 = (bf16[2,3,256,1,24,1]{2,5,4,3,1,0:T(2,128)(2,1)}, bf16[2,3,256,1,24,1]{2,5,4,3,1,0:T(2,128)(2,1)}, u32[]{:S(2)}, u32[]{:S(2)}) collective-permute-start(bf16[2,3,256,1,24,1]{2,5,4,3,1,0:T(2,128)(2,1)} %maximum_maximum_fusion.1), channel_id=1, source_target_pairs={{15,0},{0,1},{1,2},{2,3},{3,4},{4,5},{5,6},{6,7},{7,8},{8,9},{9,10... | collective-permute-start | bytes 221192 | tf_op jit(solution)/shard_map/ppermute | solution.py:19
  32.9 105.3 %collective-permute-start.4 = (bf16[2,3,256,1,24,1]{2,5,4,3,1,0:T(2,128)(2,1)}, bf16[2,3,256,1,24,1]{2,5,4,3,1,0:T(2,128)(2,1)}, u32[]{:S(2)}, u32[]{:S(2)}) collective-permute-start(bf16[2,3,256,1,24,1]{2,5,4,3,1,0:T(2,128)(2,1)} %maximum_maximum_fusion.1), channel_id=1, source_target_pairs={{3,0},{4,1},{5,2},{6,3},{7,4},{8,5},{9,6},{10,7},{11,8},{12,9},{13... | collective-permute-start | bytes 221192 | tf_op jit(solution)/shard_map/ppermute | solution.py:19
  37.1 87.8 %collective-permute-start = (bf16[2,3,256,1,1,24]{2,5,4,1,0,3:T(8,128)(2,1)}, bf16[2,3,256,1,1,24]{2,5,4,1,0,3:T(8,128)(2,1)}, u32[]{:S(2)}, u32[]{:S(2)}) collective-permute-start(bf16[2,3,256,1,1,24]{2,5,4,1,0,3:T(8,128)(2,1)} %slice.697), channel_id=1, source_target_pairs={{4,0},{5,1},{6,2},{7,3},{8,4},{9,5},{10,6},{11,7},{12,8},{13,9},{1... | collective-permute-start | bytes 221192 | tf_op jit(solution)/shard_map/ppermute | solution.py:19
  125.0 6.4 %collective-permute-start.1 = (bf16[2,3,256,1,1,24]{2,5,4,3,1,0:T(8,128)(2,1)S(1)}, bf16[2,3,256,1,1,24]{2,5,4,3,1,0:T(8,128)(2,1)S(1)}, u32[]{:S(2)}, u32[]{:S(2)}) collective-permute-start(bf16[2,3,256,1,1,24]{2,5,4,3,1,0:T(8,128)(2,1)S(1)} %maximum_maximum_fusion.2), channel_id=1, source_target_pairs={{12,0},{13,1},{14,2},{15,3},{0,4},{1,5},{2,6},{3,7},{4,8},{5,9},{6... | collective-permute-start | bytes 221192 | tf_op jit(solution)/shard_map/ppermute | solution.py:19
  131.3 11.2 %collective-permute-start.6 = (bf16[2,3,256,1,24,24]{2,5,4,1,0,3:T(8,128)(2,1)S(1)}, bf16[2,3,256,1,24,24]{2,5,4,1,0,3:T(8,128)(2,1)S(1)}, u32[]{:S(2)}, u32[]{:S(2)}) collective-permute-start(bf16[2,3,256,1,24,24]{2,5,4,1,0,3:T(8,128)(2,1)S(1)} %bitcast.630), channel_id=1, source_target_pairs={{0,0},{1,1},{2,2},{3,3},{4,4},{5,5},{6,6},{7,7},{8,8},{9,9},{10,10... | collective-permute-start | bytes 5308424 | tf_op jit(solution)/shard_map/ppermute | solution.py:19
  132.8 12.9 %collective-permute-start.7 = (bf16[2,3,256,1,24,24]{2,5,4,3,1,0:T(8,128)(2,1)S(1)}, bf16[2,3,256,1,24,24]{2,5,4,3,1,0:T(8,128)(2,1)S(1)}, u32[]{:S(2)}, u32[]{:S(2)}) collective-permute-start(bf16[2,3,256,1,24,24]{2,5,4,3,1,0:T(8,128)(2,1)S(1)} %maximum_maximum_fusion), channel_id=1, source_target_pairs={{0,0},{1,1},{2,2},{3,3},{4,4},{5,5},{6,6},{7,7},{8,8},{9,9},{10,10... | collective-permute-start | bytes 5308424 | tf_op jit(solution)/shard_map/ppermute | solution.py:19
  (108 other events, 145.6 us)
Sparse Core Ops, SparseCore 0:
  160.7 71.8 reduce-scatter.1
where the time goes:
time: 241 us; the launch traced here: 240 us
  waiting for transfers between devices  72.5 us (30%)
  local copies, waits for them, and re-layouts  60.4 us (25%)
  other arithmetic  55.4 us (23%)
  between operations  30.6 us (13%)
  starting transfers between devices  11.6 us (5%)
  matrix products  9.04 us (4%)
    reduce_scatter x1, waiting for transfers between devices, body(): lax.psum_scatter(jnp.stack(blocks, 1) * factor, 'gz', scatter_dimension=0...  72.1 us
    convert_element_type x27, local copies, waits for them, and re-layouts, apply_link(): link_imag = link_imag.astype(jnp.float32)[None, :]  24.9 us
    convert_element_type x27, local copies, waits for them, and re-layouts, apply_link(): link_real = link_real.astype(jnp.float32)[None, :]  23.7 us
    sin x8, other arithmetic, body(): sin_part = jnp.sin(phase_angle)[None, None, :]  15.3 us
    ppermute x8, starting transfers between devices, shifted(): return lax.ppermute(block, axis, route)  11.6 us
    another operation x8, other arithmetic  11 us
    dot_general x8, matrix products, body(): lax.dot_general(left_side, right_side, (((0, 1, 3), (1, 2, 4)), ((), ()))...  9.04 us
    sub x9, other arithmetic, apply_link(): sum_real = sum_real + link_real * vec_real - link_imag * vec_imag  7.26 us
  transfers between devices with their start and end apart: 9, of which 2 were waited for; matrix products, arithmetic and copies ran while one was open for 45% of the time, Pallas kernels for 0%

commit v1 on v0

v1 whole, which is shorter than its diff:
```python
import functools
import math

import jax
import jax.numpy as jnp
from jax import lax
from jax.experimental import pallas as pl
from jax.experimental.pallas import tpu as pltpu
from jax.sharding import PartitionSpec as P

NX = 96
NY = 96
ZEXT = 96

LANES = 128
EXTRA = 16
F32 = jnp.float32
BF16 = jnp.bfloat16


def route(count, shift):
    return [(i, (i + shift) % count) for i in range(count)]


def side_route(stride, sign):
    def of(i):
        here = i // stride % 4
        return i + ((here + sign) % 4 - here) * stride

    return of


def faces_kernel(side, v_ref, u_ref, low_x, high_x, low_y, high_y, rows_ref):
    sites = v_ref.shape[-1]
    count = v_ref.shape[2]
    site = lax.broadcasted_iota(jnp.int32, (sites, 4 * LANES), 0)
    lane = lax.broadcasted_iota(jnp.int32, (sites, 4 * LANES), 1)
    face = lane // LANES
    place = lane % LANES
    selectors = []
    for c in range(3):
        k = place - c * side
        wanted = jnp.where(
            face == 0,
            k,
            jnp.where(
                face == 1,
                sites - side + k,
                jnp.where(face == 2, side * k, side * k + side - 1),
            ),
        )
        hit = (site == wanted) & (k >= 0) & (k < side)
        selectors.append(jnp.where(hit, 1.0, 0.0).astype(BF16))
    outs = (low_x, high_x, low_y, high_y)
    for r in range(2):
        total = None
        for c in range(3):
            rows_ref[:count, :] = v_ref[r, c]
            pieces = []
            for d in range(2):
                pieces.append(u_ref[d, r, c].astype(F32))
                pieces.append(u_ref[d, r, :, c, :].astype(F32))
            pieces.append(jnp.zeros((EXTRA - 12, sites), F32))
            rows_ref[count:, :] = jnp.concatenate(pieces, 0).astype(BF16)
            part = jnp.dot(rows_ref[...], selectors[c], preferred_element_type=F32)
            total = part if total is None else total + part
        for f in range(4):
            piece = total[:, f * LANES : (f + 1) * LANES]
            outs[f][:, r * LANES : (r + 1) * LANES] = piece.astype(BF16)


def turn(product, extent):
    return product - extent * jnp.floor(product / extent)


def phase_rows(momenta_ref, gx, gy, gz):
    nx = momenta_ref[:, 0:1].astype(F32)
    ny = momenta_ref[:, 1:2].astype(F32)
    nz = momenta_ref[:, 2:3].astype(F32)
    total = turn(nx * gx, NX) / NX + turn(ny * gy, NY) / NY + turn(nz * gz, ZEXT) / ZEXT
    angle = 2.0 * math.pi * total
    return jnp.cos(angle), jnp.sin(angle)


def main_kernel(
    side,
    z_blocks,
    factor,
    momenta_ref,
    directions_ref,
    v_ref,
    u_ref,
    *rest,
):
    own = rest[0:4]
    halo = rest[4:8]
    rest = rest[8:]
    if z_blocks > 1:
        z_up_ref, z_down_ref, u_down_ref = rest[:3]
        rest = rest[3:]
    keep_ref, send_ref = rest[:2]
    (vp, vs, coef, disp, left, tab, edge_tab, edge_disp, edge_mat, acc) = rest[2:]
    me = lax.axis_index("gz")
    block_z = (me // 16).astype(F32)
    block_x = (me // 4 % 4).astype(F32)
    block_y = (me % 4).astype(F32)
    count = v_ref.shape[2]
    sites = v_ref.shape[3]
    wide = vp.shape[-1]
    tiles = wide // LANES
    np_ = momenta_ref.shape[0]

    lane = lax.broadcasted_iota(jnp.int32, (np_, wide), 1)
    xl = (lane // side).astype(F32)
    yl = (lane % side).astype(F32)
    c_rows, s_rows = phase_rows(
        momenta_ref, block_x * side + xl, block_y * side + yl, block_z
    )
    tab[0] = c_rows
    tab[1] = s_rows
    lane_e = lax.broadcasted_iota(jnp.int32, (np_, LANES), 1)
    k = (lane_e % side).astype(F32)
    x0 = block_x * side
    y0 = block_y * side
    last = float(side - 1)
    for f, (gx, gy) in enumerate(
        ((x0 + 0.0 * k, y0 + k), (x0 + last + 0.0 * k, y0 + k), (x0 + k, y0 + 0.0 * k), (x0 + k, y0 + last + 0.0 * k))
    ):
        c_rows, s_rows = phase_rows(momenta_ref, gx, gy, block_z)
        edge_tab[0, f] = c_rows
        edge_tab[1, f] = s_rows

    for q in range(6):
        vp[q, :, wide - LANES :] = jnp.zeros((count, LANES), BF16)
        vp[q, :, :sites] = v_ref[q // 3, q % 3]

    lane1 = lax.broadcasted_iota(jnp.int32, (1, wide), 1)
    inside = lane1 < sites

    def row(ref, d, r, i, j):
        value = ref[d, r, i, j : j + 1, :].astype(F32)
        return jnp.concatenate([value, jnp.zeros((1, wide - sites), F32)], 1)

    def put(n, value):
        coef[n] = jnp.broadcast_to(value, (8, wide))

    masks = (
        (lane1 < sites - side, (lane1 >= side) & inside),
        (inside & (lane1 % side != side - 1), inside & (lane1 % side != 0)),
    )
    for d in range(2):
        step = (side, 1)[d]
        for i in range(3):
            for j in range(3):
                for r in range(2):
                    u = row(u_ref, d, r, i, j) * 0.5
                    put(((2 * d) * 2 + r) * 9 + 3 * i + j, jnp.where(masks[d][0], u, 0.0))
                    back = pltpu.roll(u, step, 1) * (-1.0 if r == 0 else 1.0)
                    put(((2 * d + 1) * 2 + r) * 9 + 3 * j + i, jnp.where(masks[d][1], back, 0.0))
    if z_blocks > 1:
        for i in range(3):
            for j in range(3):
                for r in range(2):
                    put((8 + r) * 9 + 3 * i + j, row(u_ref, 2, r, i, j) * 0.5)
                    back = row(u_down_ref, 0, r, i, j) * (-0.5 if r == 0 else 0.5)
                    put((10 + r) * 9 + 3 * j + i, back)
    else:
        for i in range(3):
            for j in range(3):
                put(8 * 9 + 3 * i + j, 0.5 * (row(u_ref, 2, 0, i, j) - row(u_ref, 2, 0, j, i)))
                put(9 * 9 + 3 * i + j, 0.5 * (row(u_ref, 2, 1, i, j) + row(u_ref, 2, 1, j, i)))

    shifts = (wide - side, side, wide - 1, 1)

    def shift_rows(n, carry):
        rows = pl.ds(pl.multiple_of(n * 16, 16), 16)
        for q in range(6):
            value = vp[q, rows, :].astype(F32)
            for m, amount in enumerate(shifts):
                vs[m, q, rows, :] = pltpu.roll(value, amount, 1).astype(BF16)
        return carry

    lax.fori_loop(0, count // 16, shift_rows, 0)

    def pair(n, cols):
        c = coef[n, :, cols]
        return jnp.concatenate([c, c], 0)

    def apply(app, vec, cols, sums, skip_diagonal):
        for i in range(3):
            for j in range(3):
                li = pair((2 * app + 1) * 9 + 3 * i + j, cols)
                if not (skip_diagonal and i == j):
                    lr = pair((2 * app) * 9 + 3 * i + j, cols)
                    re = lr * vec[j]
                    im = lr * vec[3 + j]
                    sums[i] = re if sums[i] is None else sums[i] + re
                    sums[3 + i] = im if sums[3 + i] is None else sums[3 + i] + im
                re = li * vec[3 + j]
                im = li * vec[j]
                sums[i] = -re if sums[i] is None else sums[i] - re
                sums[3 + i] = im if sums[3 + i] is None else sums[3 + i] + im
        return sums

    def displace(n, carry):
        rows = pl.ds(pl.multiple_of(n * 16, 16), 16)

        def one_tile(t, inner):
            cols = pl.ds(pl.multiple_of(t * LANES, LANES), LANES)
            for d in range(3):
                sums = [None] * 6
                if d < 2:
                    for side_of in range(2):
                        vec = [vs[2 * d + side_of, q, rows, cols].astype(F32) for q in range(6)]
                        sums = apply(2 * d + side_of, vec, cols, sums, False)
                elif z_blocks > 1:
                    pass
                else:
                    vec = [vp[q, rows, cols].astype(F32) for q in range(6)]
                    sums = apply(4, vec, cols, sums, True)
                if d < 2 or z_blocks == 1:
                    for q in range(6):
                        at = pl.ds(pl.multiple_of((q % 3) * wide + t * LANES, LANES), LANES)
                        disp[d, q // 3, rows, at] = sums[q].astype(BF16)
            return inner

        return lax.fori_loop(0, tiles, one_tile, carry)

    lax.fori_loop(0, count // 16, displace, 0)

    if z_blocks > 1:
        for q in range(6):
            for m, ref in enumerate((z_up_ref, z_down_ref)):
                vs[m, q, :, wide - LANES :] = jnp.zeros((count, LANES), BF16)
                vs[m, q, :, :sites] = ref[q // 3, q % 3]

        def displace_z(n, carry):
            rows = pl.ds(pl.multiple_of(n * 16, 16), 16)

            def one_tile(t, inner):
                cols = pl.ds(pl.multiple_of(t * LANES, LANES), LANES)
                sums = [None] * 6
                for m in range(2):
                    vec = [vs[m, q, rows, cols].astype(F32) for q in range(6)]
                    sums = apply(4 + m, vec, cols, sums, False)
                for q in range(6):
                    at = pl.ds(pl.multiple_of((q % 3) * wide + t * LANES, LANES), LANES)
                    disp[2, q // 3, rows, at] = sums[q].astype(BF16)
                return inner

            return lax.fori_loop(0, tiles, one_tile, carry)

        lax.fori_loop(0, count // 16, displace_z, 0)

    diagonal_row = lax.broadcasted_iota(jnp.int32, (side, LANES), 0)
    diagonal_lane = lax.broadcasted_iota(jnp.int32, (side, LANES), 1)
    hit = (diagonal_lane % side == diagonal_row) & (diagonal_lane < 3 * side)
    for d in range(2):
        for f in range(2):
            source = halo[2 * d + f]
            links_of = own[2 * d + 1] if f == 0 else halo[2 * d + 1]
            first = count + 6 * d + (0 if f == 0 else 3)
            tile = links_of[count:, :].astype(F32)
            for form in range(2):
                edge_mat[...] = jnp.zeros(edge_mat.shape, BF16)
                for r in range(2):
                    for j in range(3):
                        at = first - count + j
                        ur = tile[at : at + 1, :LANES]
                        ui = tile[at : at + 1, LANES:]
                        if f == 0:
                            re, im = (ur, ui) if r == 0 else (-ui, ur)
                            scale = 0.5
                        else:
                            re, im = (ur, -ui) if r == 0 else (ui, ur)
                            scale = -0.5
                        first_half, second_half = (re, -im) if form == 0 else (im, re)
                        for h, value in enumerate((first_half, second_half)):
                            block = jnp.where(hit, value * scale, 0.0).astype(BF16)
                            edge_mat[
                                r * LANES + j * side : r * LANES + (j + 1) * side,
                                h * LANES : (h + 1) * LANES,
                            ] = block
                edge_disp[2 * d + f, form] = jnp.dot(
                    source[:count, :], edge_mat[...], preferred_element_type=F32
                ).astype(BF16)

    def dot_t(a, b):
        return lax.dot_general(a, b, (((1,), (1,)), ((), ())), preferred_element_type=F32)

    mine = me % 2
    for p in range(np_):
        d = directions_ref[p]

        def make_left(n, carry):
            rows = pl.ds(pl.multiple_of(n * 16, 16), 16)
            for t in range(tiles):
                cols = slice(t * LANES, (t + 1) * LANES)
                c = jnp.broadcast_to(tab[0, p : p + 1, cols], (16, LANES))
                s = jnp.broadcast_to(tab[1, p : p + 1, cols], (16, LANES))
                for q in range(3):
                    vr = vp[q, rows, cols].astype(F32)
                    vi = vp[3 + q, rows, cols].astype(F32)
                    at = slice(q * wide + t * LANES, q * wide + (t + 1) * LANES)
                    left[0, rows, at] = (vr * c + vi * s).astype(BF16)
                    left[1, rows, at] = (vr * s - vi * c).astype(BF16)
            return carry

        lax.fori_loop(0, count // 16, make_left, 0)
        lr = left[0]
        li = left[1]
        out_re = dot_t(lr, disp[d, 0]) - dot_t(li, disp[d, 1])
        out_im = dot_t(lr, disp[d, 1]) + dot_t(li, disp[d, 0])
        acc[0] = (out_re * factor).reshape(acc.shape[1:])
        acc[1] = (out_im * factor).reshape(acc.shape[1:])

        for axis in range(2):

            @pl.when(d == axis)
            def _():
                for f in range(2):
                    own_face = 2 * axis + 1 - f
                    c = edge_tab[0, own_face, p : p + 1, :]
                    s = edge_tab[1, own_face, p : p + 1, :]
                    tr = own[own_face][:count, :LANES].astype(F32)
                    ti = own[own_face][:count, LANES:].astype(F32)
                    el = jnp.concatenate([tr * c + ti * s, tr * s - ti * c], 1).astype(BF16)
                    for form in range(2):
                        extra = dot_t(el, edge_disp[2 * axis + f, form]) * factor
                        acc[form] = acc[form] + extra.reshape(acc.shape[1:])

        for form in range(2):
            keep_ref[p, form] = acc[form, :, mine]
            send_ref[p, form] = acc[form, :, 1 - mine].astype(BF16)


def halve(keep, send, order, me):
    count = lax.axis_size("gz")
    bits = sorted(order, reverse=True)
    bits.remove(order[0])
    for n, bit in enumerate(order):
        got = lax.ppermute(send, "gz", [(i, i ^ bit) for i in range(count)])
        total = keep + got.astype(F32)
        if n + 1 == len(order):
            return total
        following = order[n + 1]
        axis = bits.index(following)
        bits.remove(following)
        lead = total.shape[:2]
        rows = total.shape[2]
        inner = 2 ** (len(bits) - axis)
        outer = 2**axis
        tail = rows // (outer * 2 * inner)
        split = total.reshape(lead + (outer, 2, inner * tail, total.shape[-1]))
        mine = me // following % 2
        keep = lax.dynamic_index_in_dim(split, mine, 3, False)
        send = lax.dynamic_index_in_dim(split, 1 - mine, 3, False).astype(BF16)
        keep = keep.reshape(lead + (rows // 2, total.shape[-1]))
        send = send.reshape(lead + (rows // 2, total.shape[-1]))


def body(eigvecs, gauge_links, momenta, directions):
    device_count = lax.axis_size("gz")
    me = lax.axis_index("gz")
    v = eigvecs[0]
    u = gauge_links[0]
    side = NX // 4
    count, sites = v.shape[2:]
    z_blocks = device_count // 16
    if sites != side * (NY // 4) or device_count & (device_count - 1) or count % (2 * device_count) and count % device_count:
        raise ValueError("unsupported block")
    np_ = momenta.shape[0]
    factor = (3.0 * NX * NY * z_blocks) ** (-0.5)
    wide = -(-sites // LANES) * LANES
    vmem = pl.BlockSpec(memory_space=pltpu.VMEM)
    smem = pl.BlockSpec(memory_space=pltpu.SMEM)
    pack = jax.ShapeDtypeStruct((count + EXTRA, 2 * LANES), BF16)
    packs = pl.pallas_call(
        functools.partial(faces_kernel, side),
        out_shape=[pack] * 4,
        in_specs=[vmem] * 2,
        out_specs=[vmem] * 4,
        scratch_shapes=[pltpu.VMEM((count + EXTRA, sites), BF16)],
        name="faces",
    )(v, u)
    low_x, high_x, low_y, high_y = packs

    def sent(face, stride, sign):
        of = side_route(stride, sign)
        return lax.ppermute(face, "gz", [(i, of(i)) for i in range(device_count)])

    halos = [
        sent(low_x, 4, -1),
        sent(high_x, 4, 1),
        sent(low_y, 1, -1),
        sent(high_y, 1, 1),
    ]
    operands = [momenta, directions, v, u, *packs, *halos]
    specs = [vmem, smem] + [vmem] * 10
    if z_blocks > 1:
        operands += [
            lax.ppermute(v, "gz", route(device_count, -16)),
            lax.ppermute(v, "gz", route(device_count, 16)),
            lax.ppermute(u[2:3], "gz", route(device_count, 16)),
        ]
        specs += [vmem] * 3
    half = count // 2
    per = count // device_count
    applications = 6 if z_blocks > 1 else 5
    keep, send = pl.pallas_call(
        functools.partial(main_kernel, side, z_blocks, factor),
        out_shape=[
            jax.ShapeDtypeStruct((np_, 2, device_count // 2, per, count), F32),
            jax.ShapeDtypeStruct((np_, 2, device_count // 2, per, count), BF16),
        ],
        in_specs=specs,
        out_specs=[vmem] * 2,
        scratch_shapes=[
            pltpu.VMEM((6, count, wide), BF16),
            pltpu.VMEM((4, 6, count, wide), BF16),
            pltpu.VMEM((applications * 18, 8, wide), F32),
            pltpu.VMEM((3, 2, count, 3 * wide), BF16),
            pltpu.VMEM((2, count, 3 * wide), BF16),
            pltpu.VMEM((2, np_, wide), F32),
            pltpu.VMEM((2, 4, np_, LANES), F32),
            pltpu.VMEM((4, 2, count, 2 * LANES), BF16),
            pltpu.VMEM((2 * LANES, 2 * LANES), BF16),
            pltpu.VMEM((2, device_count // 2, 2, per, count), F32),
        ],
        name="products",
    )(*operands)
    keep = keep.reshape(np_, 2, half, count)
    send = send.reshape(np_, 2, half, count)
    order = [2**n for n in range(device_count.bit_length() - 1)]
    other = [order[0], order[2], order[1]] + order[3:]
    cut = np_ // 2
    first = halve(keep[:cut], send[:cut], order, me)
    second = halve(keep[cut:], send[cut:], other, me)
    return jnp.concatenate([first, second], 0)


def solution(mesh):
    return jax.shard_map(
        body,
        mesh=mesh,
        in_specs=(
            P(("slab", "gz"), None, None, None, None),
            P(("slab", "gz"), None, None, None, None, None),
            P(),
            P(),
        ),
        out_specs=P("slab", None, "gz", None),
        check_vma=False,
    )
```

time: 241 us -> 85.5 us (0.35)
  other arithmetic: 55.4 us -> 1.25 us
  waiting for transfers between devices: 72.5 us -> 19 us
  local copies, waits for them, and re-layouts: 60.4 us -> 9.53 us
  Pallas kernels: 0 us -> 39.9 us
  between operations: 30.6 us -> 0.16 us
  matrix products: 9.04 us -> 0 us
  starting transfers between devices: 11.6 us -> 15.5 us
    reduce_scatter x1 -> x0, waiting for transfers between devices: 72.1 us -> none  [body(): lax.psum_scatter(jnp.stack(blocks, 1) * factor, 'gz', scatter_dimension=0...]
    convert_element_type x54 -> x6, local copies, waits for them, and re-layouts: 48.6 us -> 0.16 us  [halve(): send = lax.dynamic_index_in_dim(split, 1 - mine, 3, False).astype(BF16)]
    pallas_call x0 -> x2, Pallas kernels: none -> 39.9 us  [the longest x1 36 us: body(): pl.pallas_call(functools.partial(main_kernel, side, z_blocks, factor), ou...]
    ppermute x8 -> x12, waiting for transfers between devices: 0.43 us -> 19 us  [the longest x8 13.1 us: halve(): got = lax.ppermute(send, 'gz', [(i, i ^ bit) for i in range(count)])]
    another operation x19 -> x0, other arithmetic: 15.9 us -> none
    sin x8 -> x0, other arithmetic: 15.3 us -> none  [body(): sin_part = jnp.sin(phase_angle)[None, None, :]]
    dot_general x8 -> x0, matrix products: 9.04 us -> none  [body(): lax.dot_general(left_side, right_side, (((0, 1, 3), (1, 2, 4)), ((), ()))...]
    convert_element_type x9 -> x0, other arithmetic: 7.61 us -> none  [the longest x3 3.04 us: apply_link(): link_imag = link_imag.astype(jnp.float32)[None, :]]
  transfers between devices with their start and end apart: 9 -> 12, of which waited for: 2 -> 9; matrix products, arithmetic and copies ran while one was open for 45% -> 2% of each run, Pallas kernels for 0% -> 0%
where the time goes in v1:
time: 85.5 us; the launch traced here: 85.3 us
  Pallas kernels  39.9 us (47%)
  waiting for transfers between devices  19 us (22%)
  starting transfers between devices  15.5 us (18%)
  local copies, waits for them, and re-layouts  9.53 us (11%)
  other arithmetic  1.25 us (1%)
    pallas_call x1, Pallas kernels, body(): pl.pallas_call(functools.partial(main_kernel, side, z_blocks, factor), ou...  36 us
    ppermute x8, waiting for transfers between devices, halve(): got = lax.ppermute(send, 'gz', [(i, i ^ bit) for i in range(count)])  13.1 us
    ppermute x8, starting transfers between devices, halve(): got = lax.ppermute(send, 'gz', [(i, i ^ bit) for i in range(count)])  9.74 us
    unnamed x17, local copies, waits for them, and re-layouts  6.63 us
    ppermute x4, waiting for transfers between devices, sent(): return lax.ppermute(face, 'gz', [(i, of(i)) for i in range(device_count)])  5.81 us
    ppermute x4, starting transfers between devices, sent(): return lax.ppermute(face, 'gz', [(i, of(i)) for i in range(device_count)])  5.74 us
    pallas_call x1, Pallas kernels, body(): pl.pallas_call(functools.partial(faces_kernel, side), out_shape=[pack] *...  3.97 us
    slice x2, local copies, waits for them, and re-layouts, body(): first = halve(keep[:cut], send[:cut], order, me)  2.62 us
  transfers between devices with their start and end apart: 12, of which 9 were waited for; matrix products, arithmetic and copies ran while one was open for 2% of the time, Pallas kernels for 0%

profile of v1, /device:TPU:0, one launch (start us, length us, event | category | flops | bytes accessed | tf_op | source)
XLA Modules:
  0.0 85.3 jit_solution(11192934498930079278)
XLA Ops:
  0.0 3.9 %copy.12 = bf16[1,2,3,256,576]{4,3,2,1,0:T(8,128)(2,1)} copy(bf16[1,2,3,256,576]{3,4,2,1,0:T(8,128)(2,1)} %param.4) | data formatting | bytes 3538944 | tf_op args[0]
  3.9 0.7 copy.26
  4.6 4.0 %faces.1 = (bf16[272,256]{1,0:T(8,128)(2,1)}, bf16[272,256]{1,0:T(8,128)(2,1)}, bf16[272,256]{1,0:T(8,128)(2,1)}, bf16[272,256]{1,0:T(8,128)(2,1)}) custom-call(bf16[2,3,256,576]{3,2,1,0:T(8,128)(2,1)} %bitcast.48, bf16[3,2,3,3,576]{4,3,2,1,0:T(4,128)(2,1)} %bitcast.58), custom_call_target="tpu_custom_call" | custom-call | tf_op jit(solution)/shard_map/faces/pallas_call | solution.py:378
  8.6 5.1 %collective-permute-start = (bf16[272,256]{1,0:T(8,128)(2,1)}, bf16[272,256]{1,0:T(8,128)(2,1)S(1)}, u32[]{:S(2)}, u32[]{:S(2)}) collective-permute-start(bf16[272,256]{1,0:T(8,128)(2,1)} %get-tuple-element.11.rest_0_), channel_id=1, source_target_pairs={{0,12},{1,13},{2,14},{3,15},{4,0},{5,1},{6,2},{7,3},{8,4},{9,5},{1... | collective-permute-start | bytes 417800 | tf_op jit(solution)/shard_map/ppermute | solution.py:390
  13.7 0.7 collective-permute-start.2
  14.3 0.7 copy.14.momenta_ref
  15.0 3.0 %collective-permute-done.rest_4_ = bf16[272,256]{1,0:T(8,128)(2,1)S(1)} collective-permute-done((bf16[272,256]{1,0:T(8,128)(2,1)}, bf16[272,256]{1,0:T(8,128)(2,1)S(1)}, u32[]{:S(2)}, u32[]{:S(2)}) %collective-permute-start) | collective-permute-done | bytes 139296 | tf_op jit(solution)/shard_map/ppermute | solution.py:390
  18.0 2.8 %collective-permute-done.1.rest_5_ = bf16[272,256]{1,0:T(8,128)(2,1)S(1)} collective-permute-done((bf16[272,256]{1,0:T(8,128)(2,1)}, bf16[272,256]{1,0:T(8,128)(2,1)S(1)}, u32[]{:S(2)}, u32[]{:S(2)}) %collective-permute-start.1) | collective-permute-done | bytes 139296 | tf_op jit(solution)/shard_map/ppermute | solution.py:390
  21.5 0.7 copy-done.4
  22.2 36.0 %products.1 = (f32[8,2,8,16,256]{4,3,2,1,0:T(8,128)}, bf16[8,2,8,16,256]{4,3,2,1,0:T(8,128)(2,1)}) custom-call(s32[8,3]{1,0:T(8,128)} %copy.14.momenta_ref, s32[8]{0:T(128)} %directions_ref.1, bf16[2,3,256,576]{3,2,1,0:T(8,128)(2,1)} %bitcast.49, bf16[3,2,3,3,576]{4,3,2,1,0:T(4,128)(2,1)} %bitcast.59, bf16[272,256]{1,0:T(8,128)(2,1)} %get-tuple-element.11.rest_0_, ...), custom_call_target="tpu_custom_call" | custom-call | tf_op jit(solution)/shard_map/products/pallas_call | solution.py:410
  58.1 2.4 %fusion.3 = (bf16[4,2,8,16,256]{4,3,2,1,0:T(8,128)(2,1)}, bf16[4,2,8,16,256]{4,3,2,1,0:T(8,128)(2,1)}) fusion(bf16[8,2,8,16,256]{4,3,2,1,0:T(8,128)(2,1)} %get-tuple-element.16), kind=kLoop, calls=%fused_computation.23 | loop fusion | bytes 2097152 | tf_op jit(solution)/shard_map/slice | solution.py:437
  61.3 1.4 %collective-permute-done.4 = bf16[4,2,128,256]{3,2,1,0:T(8,128)(2,1)S(1)} collective-permute-done((bf16[4,2,128,256]{3,2,1,0:T(8,128)(2,1)}, bf16[4,2,128,256]{3,2,1,0:T(8,128)(2,1)S(1)}, u32[]{:S(2)}, u32[]{:S(2)}) %collective-permute-start.4) | collective-permute-done | bytes 524320 | tf_op jit(solution)/shard_map/ppermute | solution.py:342
  62.7 0.7 collective-permute-done.8
  63.8 1.6 %collective-permute-start.5 = (bf16[4,2,64,256]{3,2,1,0:T(8,128)(2,1)S(1)}, bf16[4,2,64,256]{3,2,1,0:T(8,128)(2,1)S(1)}, u32[]{:S(2)}, u32[]{:S(2)}) collective-permute-start(bf16[4,2,64,256]{3,2,1,0:T(8,128)(2,1)S(1)} %bitcast.65), channel_id=1, source_target_pairs={{0,2},{1,3},{2,0},{3,1},{4,6},{5,7},{6,4},{7,5},{8,10},{9,11},{10,... | collective-permute-start | bytes 786440 | tf_op jit(solution)/shard_map/ppermute | solution.py:342
  65.4 1.6 %collective-permute-start.9 = (bf16[4,2,64,256]{3,2,1,0:T(8,128)(2,1)S(1)}, bf16[4,2,64,256]{3,2,1,0:T(8,128)(2,1)S(1)}, u32[]{:S(2)}, u32[]{:S(2)}) collective-permute-start(bf16[4,2,64,256]{3,2,1,0:T(8,128)(2,1)S(1)} %bitcast.64), channel_id=1, source_target_pairs={{0,4},{1,5},{2,6},{3,7},{4,0},{5,1},{6,2},{7,3},{8,12},{9,13},{10,... | collective-permute-start | bytes 786440 | tf_op jit(solution)/shard_map/ppermute | solution.py:342
  67.1 5.2 %collective-permute-done.5 = bf16[4,2,64,256]{3,2,1,0:T(8,128)(2,1)S(1)} collective-permute-done((bf16[4,2,64,256]{3,2,1,0:T(8,128)(2,1)S(1)}, bf16[4,2,64,256]{3,2,1,0:T(8,128)(2,1)S(1)}, u32[]{:S(2)}, u32[]{:S(2)}) %collective-permute-start.5) | collective-permute-done | bytes 262176 | tf_op jit(solution)/shard_map/ppermute | solution.py:342
  72.3 1.6 %collective-permute-start.6 = (bf16[4,2,32,256]{3,2,1,0:T(8,128)(2,1)S(1)}, bf16[4,2,32,256]{3,2,1,0:T(8,128)(2,1)S(1)}, u32[]{:S(2)}, u32[]{:S(2)}) collective-permute-start(bf16[4,2,32,256]{3,2,1,0:T(8,128)(2,1)S(1)} %bitcast.66), channel_id=1, source_target_pairs={{0,4},{1,5},{2,6},{3,7},{4,0},{5,1},{6,2},{7,3},{8,12},{9,13},{10,... | collective-permute-start | bytes 393224 | tf_op jit(solution)/shard_map/ppermute | solution.py:342
  74.0 1.6 %collective-permute-start.10 = (bf16[4,2,32,256]{3,2,1,0:T(8,128)(2,1)S(1)}, bf16[4,2,32,256]{3,2,1,0:T(8,128)(2,1)S(1)}, u32[]{:S(2)}, u32[]{:S(2)}) collective-permute-start(bf16[4,2,32,256]{3,2,1,0:T(8,128)(2,1)S(1)} %bitcast.67), channel_id=1, source_target_pairs={{0,2},{1,3},{2,0},{3,1},{4,6},{5,7},{6,4},{7,5},{8,10},{9,11},{10,... | collective-permute-start | bytes 393224 | tf_op jit(solution)/shard_map/ppermute | solution.py:342
  75.6 1.7 %collective-permute-done.6 = bf16[4,2,32,256]{3,2,1,0:T(8,128)(2,1)S(1)} collective-permute-done((bf16[4,2,32,256]{3,2,1,0:T(8,128)(2,1)S(1)}, bf16[4,2,32,256]{3,2,1,0:T(8,128)(2,1)S(1)}, u32[]{:S(2)}, u32[]{:S(2)}) %collective-permute-start.6) | collective-permute-done | bytes 131104 | tf_op jit(solution)/shard_map/ppermute | solution.py:342
  77.4 1.3 %collective-permute-start.7 = (bf16[4,2,16,256]{3,2,1,0:T(8,128)(2,1)S(1)}, bf16[4,2,16,256]{3,2,1,0:T(8,128)(2,1)S(1)}, u32[]{:S(2)}, u32[]{:S(2)}) collective-permute-start(bf16[4,2,16,256]{3,2,1,0:T(8,128)(2,1)S(1)} %fusion), channel_id=1, source_target_pairs={{0,8},{1,9},{2,10},{3,11},{4,12},{5,13},{6,14},{7,15},{8,0},{9,1},... | collective-permute-start | bytes 196616 | tf_op jit(solution)/shard_map/ppermute | solution.py:342
  79.1 1.6 %collective-permute-start.11 = (bf16[4,2,16,256]{3,2,1,0:T(8,128)(2,1)S(1)}, bf16[4,2,16,256]{3,2,1,0:T(8,128)(2,1)S(1)}, u32[]{:S(2)}, u32[]{:S(2)}) collective-permute-start(bf16[4,2,16,256]{3,2,1,0:T(8,128)(2,1)S(1)} %fusion.1), channel_id=1, source_target_pairs={{0,8},{1,9},{2,10},{3,11},{4,12},{5,13},{6,14},{7,15},{8,0},{9,1},... | collective-permute-start | bytes 196616 | tf_op jit(solution)/shard_map/ppermute | solution.py:342
  80.8 3.1 %collective-permute-done.7 = bf16[4,2,16,256]{3,2,1,0:T(8,128)(2,1)S(1)} collective-permute-done((bf16[4,2,16,256]{3,2,1,0:T(8,128)(2,1)S(1)}, bf16[4,2,16,256]{3,2,1,0:T(8,128)(2,1)S(1)}, u32[]{:S(2)}, u32[]{:S(2)}) %collective-permute-start.7) | collective-permute-done | bytes 65568 | tf_op jit(solution)/shard_map/ppermute | solution.py:342
  83.9 0.7 collective-permute-done.11
  84.6 0.7 pad_maximum_fusion
  (39 shorter events, 2.5 us)
Async XLA Ops:
  0.0 3.9 %copy-start.5 = (bf16[1,3,2,3,3,576]{5,2,4,3,1,0:T(2,128)(2,1)S(1)}, bf16[1,3,2,3,3,576]{5,2,4,3,1,0:T(2,128)(2,1)}, u32[]{:S(2)}) copy-start(bf16[1,3,2,3,3,576]{5,2,4,3,1,0:T(2,128)(2,1)} %param.5) | copy-start | bytes 186628
  0.0 14.3 %copy-start.6 = (s32[8,3]{0,1:T(4,128)S(1)}, s32[8,3]{0,1:T(4,128)}, u32[]{:S(2)}) copy-start(s32[8,3]{0,1:T(4,128)} %param.6) | copy-start | bytes 292
  8.6 9.5 %collective-permute-start = (bf16[272,256]{1,0:T(8,128)(2,1)}, bf16[272,256]{1,0:T(8,128)(2,1)S(1)}, u32[]{:S(2)}, u32[]{:S(2)}) collective-permute-start(bf16[272,256]{1,0:T(8,128)(2,1)} %get-tuple-element.11.rest_0_), channel_id=1, source_target_pairs={{0,12},{1,13},{2,14},{3,15},{4,0},{5,1},{6,2},{7,3},{8,4},{9,5},{1... | collective-permute-start | bytes 417800 | tf_op jit(solution)/shard_map/ppermute | solution.py:390
  13.7 7.1 %collective-permute-start.1 = (bf16[272,256]{1,0:T(8,128)(2,1)}, bf16[272,256]{1,0:T(8,128)(2,1)S(1)}, u32[]{:S(2)}, u32[]{:S(2)}) collective-permute-start(bf16[272,256]{1,0:T(8,128)(2,1)} %get-tuple-element.12.rest_1_), channel_id=1, source_target_pairs={{0,4},{1,5},{2,6},{3,7},{4,8},{5,9},{6,10},{7,11},{8,12},{9,13},{1... | collective-permute-start | bytes 417800 | tf_op jit(solution)/shard_map/ppermute | solution.py:390
  13.7 7.1 %collective-permute-start.2 = (bf16[272,256]{1,0:T(8,128)(2,1)}, bf16[272,256]{1,0:T(8,128)(2,1)S(1)}, u32[]{:S(2)}, u32[]{:S(2)}) collective-permute-start(bf16[272,256]{1,0:T(8,128)(2,1)} %get-tuple-element.13.rest_2_), channel_id=1, source_target_pairs={{0,3},{1,0},{2,1},{3,2},{4,7},{5,4},{6,5},{7,6},{8,11},{9,8},{10,9... | collective-permute-start | bytes 417800 | tf_op jit(solution)/shard_map/ppermute | solution.py:390
  14.3 6.5 %collective-permute-start.3 = (bf16[272,256]{1,0:T(8,128)(2,1)}, bf16[272,256]{1,0:T(8,128)(2,1)S(1)}, u32[]{:S(2)}, u32[]{:S(2)}) collective-permute-start(bf16[272,256]{1,0:T(8,128)(2,1)} %get-tuple-element.14.rest_3_), channel_id=1, source_target_pairs={{0,1},{1,2},{2,3},{3,0},{4,5},{5,6},{6,7},{7,4},{8,9},{9,10},{10,1... | collective-permute-start | bytes 417800 | tf_op jit(solution)/shard_map/ppermute | solution.py:390
  18.0 2.8 %copy-start.1 = (bf16[272,256]{1,0:T(8,128)(2,1)}, bf16[272,256]{1,0:T(8,128)(2,1)S(1)}, u32[]{:S(2)}) copy-start(bf16[272,256]{1,0:T(8,128)(2,1)S(1)} %collective-permute-done.rest_4_) | copy-start | bytes 417796
  20.8 0.7 copy-start.2
  20.8 0.7 copy-start.3
  21.5 0.7 copy-start.4
  58.1 2.9 %copy-start = (f32[8,2,8,16,256]{4,3,2,1,0:T(8,128)S(1)}, f32[8,2,8,16,256]{4,3,2,1,0:T(8,128)}, u32[]{:S(2)}) copy-start(f32[8,2,8,16,256]{4,3,2,1,0:T(8,128)} %get-tuple-element.15) | copy-start | bytes 6291460
  60.6 2.1 %collective-permute-start.4 = (bf16[4,2,128,256]{3,2,1,0:T(8,128)(2,1)}, bf16[4,2,128,256]{3,2,1,0:T(8,128)(2,1)S(1)}, u32[]{:S(2)}, u32[]{:S(2)}) collective-permute-start(bf16[4,2,128,256]{3,2,1,0:T(8,128)(2,1)} %bitcast.3), channel_id=1, source_target_pairs={{0,1},{1,0},{2,3},{3,2},{4,5},{5,4},{6,7},{7,6},{8,9},{9,8},{10,11... | collective-permute-start | bytes 1572872 | tf_op jit(solution)/shard_map/ppermute | solution.py:342
  60.6 2.9 %collective-permute-start.8 = (bf16[4,2,128,256]{3,2,1,0:T(8,128)(2,1)}, bf16[4,2,128,256]{3,2,1,0:T(8,128)(2,1)S(1)}, u32[]{:S(2)}, u32[]{:S(2)}) collective-permute-start(bf16[4,2,128,256]{3,2,1,0:T(8,128)(2,1)} %bitcast.14), channel_id=1, source_target_pairs={{0,1},{1,0},{2,3},{3,2},{4,5},{5,4},{6,7},{7,6},{8,9},{9,8},{10,11... | collective-permute-start | bytes 1572872 | tf_op jit(solution)/shard_map/ppermute | solution.py:342
  63.8 8.4 %collective-permute-start.5 = (bf16[4,2,64,256]{3,2,1,0:T(8,128)(2,1)S(1)}, bf16[4,2,64,256]{3,2,1,0:T(8,128)(2,1)S(1)}, u32[]{:S(2)}, u32[]{:S(2)}) collective-permute-start(bf16[4,2,64,256]{3,2,1,0:T(8,128)(2,1)S(1)} %bitcast.65), channel_id=1, source_target_pairs={{0,2},{1,3},{2,0},{3,1},{4,6},{5,7},{6,4},{7,5},{8,10},{9,11},{10,... | collective-permute-start | bytes 786440 | tf_op jit(solution)/shard_map/ppermute | solution.py:342
  65.4 8.5 %collective-permute-start.9 = (bf16[4,2,64,256]{3,2,1,0:T(8,128)(2,1)S(1)}, bf16[4,2,64,256]{3,2,1,0:T(8,128)(2,1)S(1)}, u32[]{:S(2)}, u32[]{:S(2)}) collective-permute-start(bf16[4,2,64,256]{3,2,1,0:T(8,128)(2,1)S(1)} %bitcast.64), channel_id=1, source_target_pairs={{0,4},{1,5},{2,6},{3,7},{4,0},{5,1},{6,2},{7,3},{8,12},{9,13},{10,... | collective-permute-start | bytes 786440 | tf_op jit(solution)/shard_map/ppermute | solution.py:342
  72.3 5.0 %collective-permute-start.6 = (bf16[4,2,32,256]{3,2,1,0:T(8,128)(2,1)S(1)}, bf16[4,2,32,256]{3,2,1,0:T(8,128)(2,1)S(1)}, u32[]{:S(2)}, u32[]{:S(2)}) collective-permute-start(bf16[4,2,32,256]{3,2,1,0:T(8,128)(2,1)S(1)} %bitcast.66), channel_id=1, source_target_pairs={{0,4},{1,5},{2,6},{3,7},{4,0},{5,1},{6,2},{7,3},{8,12},{9,13},{10,... | collective-permute-start | bytes 393224 | tf_op jit(solution)/shard_map/ppermute | solution.py:342
  74.0 5.0 %collective-permute-start.10 = (bf16[4,2,32,256]{3,2,1,0:T(8,128)(2,1)S(1)}, bf16[4,2,32,256]{3,2,1,0:T(8,128)(2,1)S(1)}, u32[]{:S(2)}, u32[]{:S(2)}) collective-permute-start(bf16[4,2,32,256]{3,2,1,0:T(8,128)(2,1)S(1)} %bitcast.67), channel_id=1, source_target_pairs={{0,2},{1,3},{2,0},{3,1},{4,6},{5,7},{6,4},{7,5},{8,10},{9,11},{10,... | collective-permute-start | bytes 393224 | tf_op jit(solution)/shard_map/ppermute | solution.py:342
  77.4 6.4 %collective-permute-start.7 = (bf16[4,2,16,256]{3,2,1,0:T(8,128)(2,1)S(1)}, bf16[4,2,16,256]{3,2,1,0:T(8,128)(2,1)S(1)}, u32[]{:S(2)}, u32[]{:S(2)}) collective-permute-start(bf16[4,2,16,256]{3,2,1,0:T(8,128)(2,1)S(1)} %fusion), channel_id=1, source_target_pairs={{0,8},{1,9},{2,10},{3,11},{4,12},{5,13},{6,14},{7,15},{8,0},{9,1},... | collective-permute-start | bytes 196616 | tf_op jit(solution)/shard_map/ppermute | solution.py:342
  79.1 5.4 %collective-permute-start.11 = (bf16[4,2,16,256]{3,2,1,0:T(8,128)(2,1)S(1)}, bf16[4,2,16,256]{3,2,1,0:T(8,128)(2,1)S(1)}, u32[]{:S(2)}, u32[]{:S(2)}) collective-permute-start(bf16[4,2,16,256]{3,2,1,0:T(8,128)(2,1)S(1)} %fusion.1), channel_id=1, source_target_pairs={{0,8},{1,9},{2,10},{3,11},{4,12},{5,13},{6,14},{7,15},{8,0},{9,1},... | collective-permute-start | bytes 196616 | tf_op jit(solution)/shard_map/ppermute | solution.py:342

commit v2 on v0

v2 whole, which is shorter than its diff:
```python
import functools
import math

import jax
import jax.numpy as jnp
from jax import lax
from jax.experimental import pallas as pl
from jax.experimental.pallas import tpu as pltpu
from jax.sharding import PartitionSpec as P

NX = 96
NY = 96
ZEXT = 96

LANES = 128
EXTRA = 32
VMEM_LIMIT = 30 * 2**20
F32 = jnp.float32
BF16 = jnp.bfloat16


def route(count, shift):
    return [(i, (i + shift) % count) for i in range(count)]


def side_route(stride, sign):
    def of(i):
        here = i // stride % 4
        return i + ((here + sign) % 4 - here) * stride

    return of


def wide_row(rows, wide):
    pad = jnp.zeros((rows.shape[0], wide - rows.shape[1]), F32)
    return jnp.concatenate([rows, pad], 1)


def link_rows(ref, d):
    return jnp.concatenate([ref[d, i, j].astype(F32) for i in range(3) for j in range(3)], 0)


def faces_kernel(side, place, v_ref, u_ref, low_x, high_x, low_y, high_y, near_ref, v32):
    sites = v_ref.shape[2]
    last = side - 1
    for q in range(6):
        rows = pl.ds(q * side, side)
        low_x[rows, :] = v_ref[q // 3, q % 3, :side, :]
        high_x[rows, :] = v_ref[q // 3, q % 3, sites - side :, :]
        for h in range(v32.shape[0]):
            at = slice(h * LANES, (h + 1) * LANES)
            v32[h] = v_ref[q // 3, q % 3, :, at].astype(F32)
            low_y[rows, at] = v32[h, pl.ds(0, side, stride=side), :].astype(BF16)
            high_y[rows, at] = v32[h, pl.ds(last, side, stride=side), :].astype(BF16)
    site = lax.broadcasted_iota(jnp.int32, (sites, LANES), 0)
    lane = lax.broadcasted_iota(jnp.int32, (sites, LANES), 1)
    k = lane - place
    wanted_y = jnp.where(k < side, k, k - side) * side + last
    wanted = jnp.where(lane < side, sites - side + lane, wanted_y)
    hit = (site == wanted) & ((lane < side) | ((k >= 0) & (k < 2 * side)))
    pick = jnp.where(hit, 1.0, 0.0).astype(BF16)
    rest = jnp.zeros((EXTRA - 18, LANES), F32)
    for d, out in enumerate((high_x, high_y)):
        rows = link_rows(u_ref, d).astype(BF16)
        taken = jnp.dot(rows, pick, preferred_element_type=F32)
        taken = jnp.concatenate([taken, rest], 0).astype(BF16)
        out[6 * side :, :] = jnp.concatenate([taken, taken], 1)
        if d == 1:
            near_ref[...] = taken


def turn(product, extent):
    return product - extent * jnp.floor(product / extent)


def phase_rows(momenta_ref, gx, gy, gz):
    nx = momenta_ref[:, 0:1].astype(F32)
    ny = momenta_ref[:, 1:2].astype(F32)
    nz = momenta_ref[:, 2:3].astype(F32)
    total = turn(nx * gx, NX) / NX + turn(ny * gy, NY) / NY + turn(nz * gz, ZEXT) / ZEXT
    angle = 2.0 * math.pi * total
    return jnp.cos(angle), jnp.sin(angle)


def put(coef, app, i, j, re, im):
    for n, value in enumerate((re, im, re + im)):
        coef[app * 27 + n * 9 + 3 * i + j] = jnp.broadcast_to(value, coef.shape[1:])


def place_of(q, t, tiles):
    inner = tiles - 2
    if 0 < t < tiles - 1:
        return q * inner + t - 1
    return 3 * inner + q * 2 + (t > 0)


def displace_tile(apps, skip_diagonal=False):
    def pair(links, app, n, i, j, cols):
        c = links[app * 27 + n * 9 + 3 * i + j, :, cols]
        return jnp.concatenate([c, c], 0)

    def add(a, b):
        return b if a is None else a + b

    joined = [[vec[j] + vec[3 + j] for j in range(3)] for _, _, _, vec in apps]
    out = [None] * 6
    for i in range(3):
        p1 = p2 = p3 = None
        for (links, app, cols, vec), both in zip(apps, joined):
            for j in range(3):
                if not (skip_diagonal and i == j):
                    p1 = add(p1, pair(links, app, 0, i, j, cols) * vec[j])
                p2 = add(p2, pair(links, app, 1, i, j, cols) * vec[3 + j])
                p3 = add(p3, pair(links, app, 2, i, j, cols) * both[j])
        out[i] = p1 - p2
        out[3 + i] = p3 - p1 - p2
    return out


def store_tile(ref, d, n, q_places, count, values):
    for q in range(6):
        rows = pl.ds(pl.multiple_of((q // 3) * count + n * 16, 16), 16)
        at = slice(q_places[q % 3] * LANES, (q_places[q % 3] + 1) * LANES)
        ref[d, rows, at] = values[q].astype(BF16)


def interior_kernel(side, z_blocks, momenta_ref, v_ref, u_ref, low_y, high_y, *rest):
    if z_blocks > 1:
        z_up_ref, z_down_ref, u_down_ref = rest[:3]
        rest = rest[3:]
        vz = rest[3]
        rest = rest[:3] + rest[4:]
    vp, tab, coef, inner_ref, vs = rest[0], rest[1], rest[2], rest[3], rest[4]
    me = lax.axis_index("gz")
    block_z = (me // 16).astype(F32)
    block_x = (me // 4 % 4).astype(F32)
    block_y = (me % 4).astype(F32)
    sites = v_ref.shape[2]
    count = v_ref.shape[3]
    wide = vp.shape[-1]
    tiles = wide // LANES
    np_ = momenta_ref.shape[0]

    lane = lax.broadcasted_iota(jnp.int32, (np_, wide), 1)
    behind = lane - sites
    on_face = behind >= 0
    xl = jnp.where(on_face, behind % side, lane // side).astype(F32)
    yl = jnp.where(on_face, jnp.where(behind < side, side - 1, 0), lane % side).astype(F32)
    c_rows, s_rows = phase_rows(momenta_ref, block_x * side + xl, block_y * side + yl, block_z)
    tab[0] = c_rows
    tab[1] = s_rows

    for q in range(6):
        at = slice(q * side, (q + 1) * side)
        pieces = [
            v_ref[q // 3, q % 3].astype(F32),
            high_y[at, :].astype(F32),
            low_y[at, :].astype(F32),
            jnp.zeros((wide - sites - 2 * side, count), F32),
        ]
        vp[q] = jnp.concatenate(pieces, 0).T.astype(BF16)

    lane1 = lax.broadcasted_iota(jnp.int32, (1, wide), 1)
    inside = lane1 < sites
    masks = (
        (inside, inside & (lane1 >= side)),
        (inside & (lane1 % side != side - 1), inside & (lane1 % side != 0)),
    )
    for d in range(2):
        rows = wide_row(link_rows(u_ref, d) * 0.5, wide)
        ahead = jnp.where(masks[d][0], rows, 0.0)
        back = jnp.where(masks[d][1], pltpu.roll(rows, (side, 1)[d], 1), 0.0)
        for i in range(3):
            for j in range(3):
                n = (3 * i + j) * 2
                put(coef, 2 * d, i, j, ahead[n : n + 1], ahead[n + 1 : n + 2])
                put(coef, 2 * d + 1, j, i, -back[n : n + 1], back[n + 1 : n + 2])
    rows = wide_row(link_rows(u_ref, 2) * 0.5, wide)
    if z_blocks > 1:
        back = wide_row(link_rows(u_down_ref, 0) * 0.5, wide)
    for i in range(3):
        for j in range(3):
            n = (3 * i + j) * 2
            m = (3 * j + i) * 2
            if z_blocks > 1:
                put(coef, 4, i, j, rows[n : n + 1], rows[n + 1 : n + 2])
                put(coef, 5, j, i, -back[n : n + 1], back[n + 1 : n + 2])
            else:
                put(coef, 4, i, j, rows[n : n + 1] - rows[m : m + 1], rows[n + 1 : n + 2] + rows[m + 1 : m + 2])
    if z_blocks > 1:
        for q in range(6):
            for m, ref in enumerate((z_up_ref, z_down_ref)):
                value = ref[q // 3, q % 3].astype(F32)
                value = jnp.concatenate([value, jnp.zeros((wide - sites, count), F32)], 0)
                vz[m, q] = value.T.astype(BF16)

    shifts = (wide - side, side, wide - 1, 1)

    def displace(n, carry):
        rows = pl.ds(pl.multiple_of(n * 16, 16), 16)
        for q in range(6):
            value = vp[q, rows, :].astype(F32)
            for m, amount in enumerate(shifts):
                vs[m, q] = pltpu.roll(value, amount, 1)
        for t in range(1, tiles - 1):
            cols = slice(t * LANES, (t + 1) * LANES)
            spots = [place_of(q, t, tiles) for q in range(3)]
            for d in range(2):
                apps = [(coef, 2 * d + m, cols, [vs[2 * d + m, q, :, cols] for q in range(6)]) for m in range(2)]
                store_tile(inner_ref, d, n, spots, count, displace_tile(apps))
            if z_blocks == 1:
                vec = [vp[q, rows, cols].astype(F32) for q in range(6)]
                values = displace_tile([(coef, 4, cols, vec)], True)
            else:
                apps = [(coef, 4 + m, cols, [vz[m, q, rows, cols].astype(F32) for q in range(6)]) for m in range(2)]
                values = displace_tile(apps)
            store_tile(inner_ref, 2, n, spots, count, values)
        return carry

    lax.fori_loop(0, count // 16, displace, 0)


def border(side, sites, vp, vz, coef, near_ref, halo, outer, halo_t, side_coef):
    up_x, down_x, up_y, down_y = halo
    count = vp.shape[1]
    wide = vp.shape[-1]
    tiles = wide // LANES
    tail = sites - (tiles - 1) * LANES
    first = slice(0, LANES)
    final = slice((tiles - 1) * LANES, wide)
    for q in range(6):
        at = slice(q * side, (q + 1) * side)
        pieces = [
            down_x[at, :].astype(F32),
            jnp.zeros((tail - 2 * side, count), F32),
            up_x[at, :].astype(F32),
            up_y[at, :].astype(F32),
            down_y[at, :].astype(F32),
            jnp.zeros((LANES - tail - 2 * side, count), F32),
        ]
        halo_t[q] = jnp.concatenate(pieces, 0).T.astype(BF16)
    lane = lax.broadcasted_iota(jnp.int32, (1, LANES), 1)
    rows_x = down_x[6 * side :, :LANES].astype(F32) * 0.5
    rows_y = down_y[6 * side :, :LANES].astype(F32) * 0.5
    near = near_ref[...].astype(F32) * 0.5
    up_lanes = (lane >= tail) & (lane < tail + side)
    down_lanes = (lane >= tail + side) & (lane < tail + 2 * side)
    for i in range(3):
        for j in range(3):
            n = (3 * i + j) * 2
            m = (3 * j + i) * 2
            re = jnp.where(lane < side, -rows_x[m : m + 1], coef[27 + 3 * i + j, 0:1, first])
            im = jnp.where(lane < side, rows_x[m + 1 : m + 2], coef[27 + 9 + 3 * i + j, 0:1, first])
            put(side_coef, 0, i, j, re, im)
            re = jnp.where(up_lanes, near[n : n + 1], jnp.where(down_lanes, -rows_y[m : m + 1], 0.0))
            im = jnp.where(up_lanes, near[n + 1 : n + 2], jnp.where(down_lanes, rows_y[m + 1 : m + 2], 0.0))
            put(side_coef, 1, i, j, re, im)

    lane16 = lax.broadcasted_iota(jnp.int32, (16, LANES), 1)
    alone = slice(0, LANES)
    base = 3 * (tiles - 2)

    def one(n, carry):
        rows = pl.ds(pl.multiple_of(n * 16, 16), 16)
        got = [halo_t[q, rows, :].astype(F32) for q in range(6)]
        start = [vp[q, rows, 0 : 2 * LANES].astype(F32) for q in range(6)]
        spots = [place_of(q, 0, tiles) - base for q in range(3)]
        ahead = [pltpu.roll(a, 2 * LANES - side, 1)[:, :LANES] for a in start]
        behind = [jnp.where(lane16 < side, g, pltpu.roll(a[:, :LANES], side, 1)) for a, g in zip(start, got)]
        store_tile(outer, 0, n, spots, count, displace_tile([(coef, 0, first, ahead), (side_coef, 0, alone, behind)]))
        ahead = [pltpu.roll(a, 2 * LANES - 1, 1)[:, :LANES] for a in start]
        behind = [pltpu.roll(a[:, :LANES], 1, 1) for a in start]
        store_tile(outer, 1, n, spots, count, displace_tile([(coef, 2, first, ahead), (coef, 3, first, behind)]))
        if vz is None:
            values = displace_tile([(coef, 4, first, [a[:, :LANES] for a in start])], True)
        else:
            values = displace_tile([(coef, 4 + m, first, [vz[m, q, rows, first].astype(F32) for q in range(6)]) for m in range(2)])
        store_tile(outer, 2, n, spots, count, values)

        end = [vp[q, rows, wide - 2 * LANES : wide].astype(F32) for q in range(6)]
        spots = [place_of(q, tiles - 1, tiles) - base for q in range(3)]
        ahead = [jnp.where(lane16 >= tail - side, g, pltpu.roll(a[:, LANES:], LANES - side, 1)) for a, g in zip(end, got)]
        behind = [pltpu.roll(a, side, 1)[:, LANES:] for a in end]
        store_tile(outer, 0, n, spots, count, displace_tile([(coef, 0, final, ahead), (coef, 1, final, behind)]))
        ahead = [pltpu.roll(a[:, LANES:], LANES - 1, 1) for a in end]
        behind = [pltpu.roll(a, 1, 1)[:, LANES:] for a in end]
        apps = [(coef, 2, final, ahead), (coef, 3, final, behind), (side_coef, 1, alone, got)]
        store_tile(outer, 1, n, spots, count, displace_tile(apps))
        if vz is None:
            values = displace_tile([(coef, 4, final, [a[:, LANES:] for a in end])], True)
        else:
            values = displace_tile([(coef, 4 + m, final, [vz[m, q, rows, final].astype(F32) for q in range(6)]) for m in range(2)])
        store_tile(outer, 2, n, spots, count, values)
        return carry

    lax.fori_loop(0, count // 16, one, 0)


def products_kernel(side, sites, z_blocks, factor, start, stop, with_border, directions_ref, vp, tab, inner_ref, *rest):
    me = lax.axis_index("gz")
    if with_border:
        coef, near_ref = rest[:2]
        halo = rest[2:6]
        rest = rest[6:]
        vz = None
        if z_blocks > 1:
            vz = rest[0]
            rest = rest[1:]
        keep_ref, send_ref, outer = rest[:3]
        left, acc, halo_t, side_coef = rest[3:]
        border(side, sites, vp, vz, coef, near_ref, halo, outer, halo_t, side_coef)
    else:
        outer = rest[0]
        keep_ref, send_ref, left, acc = rest[1:]
    count = vp.shape[1]
    tiles = vp.shape[2] // LANES
    cut = 3 * (tiles - 2) * LANES
    mine = me % 2

    def dot_t(a, b):
        return lax.dot_general(a, b, (((1,), (1,)), ((), ())), preferred_element_type=F32)

    for p in range(start, stop):
        d = directions_ref[p]

        def make_left(n, carry):
            rows = pl.ds(pl.multiple_of(n * 16, 16), 16)
            lower = pl.ds(pl.multiple_of(count + n * 16, 16), 16)
            for t in range(tiles):
                cols = slice(t * LANES, (t + 1) * LANES)
                c = jnp.broadcast_to(tab[0, p : p + 1, cols], (16, LANES))
                s = jnp.broadcast_to(tab[1, p : p + 1, cols], (16, LANES))
                for q in range(3):
                    vr = vp[q, rows, cols].astype(F32)
                    vi = vp[3 + q, rows, cols].astype(F32)
                    spot = place_of(q, t, tiles)
                    at = slice(spot * LANES, (spot + 1) * LANES)
                    left[rows, at] = (vr * c + vi * s).astype(BF16)
                    left[lower, at] = (vr * s - vi * c).astype(BF16)
            return carry

        lax.fori_loop(0, count // 16, make_left, 0)
        both = dot_t(left[:, :cut], inner_ref[d]) + dot_t(left[:, cut:], outer[d])
        out_re = both[:count, :count] - both[count:, count:]
        out_im = both[:count, count:] + both[count:, :count]
        acc[0] = (out_re * factor).reshape(acc.shape[1:])
        acc[1] = (out_im * factor).reshape(acc.shape[1:])
        for form in range(2):
            keep_ref[p - start, form] = acc[form, :, mine]
            send_ref[p - start, form] = acc[form, :, 1 - mine].astype(BF16)


def halve(keep, send, order, me):
    count = lax.axis_size("gz")
    bits = sorted(order, reverse=True)
    bits.remove(order[0])
    for n, bit in enumerate(order):
        got = lax.ppermute(send, "gz", [(i, i ^ bit) for i in range(count)])
        total = keep + got.astype(F32)
        if n + 1 == len(order):
            return total
        following = order[n + 1]
        axis = bits.index(following)
        bits.remove(following)
        lead = total.shape[:2]
        rows = total.shape[2]
        inner = 2 ** (len(bits) - axis)
        outer = 2**axis
        tail = rows // (outer * 2 * inner)
        split = total.reshape(lead + (outer, 2, inner * tail, total.shape[-1]))
        mine = me // following % 2
        keep = lax.dynamic_index_in_dim(split, mine, 3, False)
        send = lax.dynamic_index_in_dim(split, 1 - mine, 3, False).astype(BF16)
        keep = keep.reshape(lead + (rows // 2, total.shape[-1]))
        send = send.reshape(lead + (rows // 2, total.shape[-1]))


def body(eigvecs, gauge_links, momenta, directions):
    device_count = lax.axis_size("gz")
    me = lax.axis_index("gz")
    v = jnp.swapaxes(eigvecs[0], 2, 3)
    u = jnp.transpose(gauge_links[0], (0, 2, 3, 1, 4))
    side = NX // 4
    sites, count = v.shape[2:]
    z_blocks = device_count // 16
    wide = -(-sites // LANES) * LANES
    tiles = wide // LANES
    tail = sites - wide + LANES
    if sites != side * (NY // 4) or device_count & (device_count - 1) or count % device_count:
        raise ValueError("unsupported block")
    if tiles < 3 or tail < 2 * side or tail + 2 * side > LANES:
        raise ValueError("unsupported sites")
    np_ = momenta.shape[0]
    factor = (3.0 * NX * NY * z_blocks) ** (-0.5)
    vmem = pl.BlockSpec(memory_space=pltpu.VMEM)
    smem = pl.BlockSpec(memory_space=pltpu.SMEM)
    params = pltpu.CompilerParams(vmem_limit_bytes=VMEM_LIMIT)
    low = jax.ShapeDtypeStruct((6 * side, count), BF16)
    high = jax.ShapeDtypeStruct((6 * side + EXTRA, count), BF16)
    low_x, high_x, low_y, high_y, near = pl.pallas_call(
        functools.partial(faces_kernel, side, tail),
        out_shape=[low, high, low, high, jax.ShapeDtypeStruct((EXTRA, LANES), BF16)],
        in_specs=[vmem] * 2,
        out_specs=[vmem] * 5,
        scratch_shapes=[pltpu.VMEM((count // LANES, sites, LANES), F32)],
        compiler_params=params,
        name="faces",
    )(v, u)

    def sent(face, stride, sign):
        of = side_route(stride, sign)
        return lax.ppermute(face, "gz", [(i, of(i)) for i in range(device_count)])

    halos = [
        sent(low_x, 4, -1),
        sent(high_x, 4, 1),
        sent(low_y, 1, -1),
        sent(high_y, 1, 1),
    ]
    applications = 6 if z_blocks > 1 else 5
    operands = [momenta, v, u, low_y, high_y]
    moved = jax.ShapeDtypeStruct((6, count, wide), BF16)
    shapes = [
        moved,
        jax.ShapeDtypeStruct((2, np_, wide), F32),
        jax.ShapeDtypeStruct((applications * 27, 8, wide), F32),
    ]
    if z_blocks > 1:
        operands += [
            lax.ppermute(v, "gz", route(device_count, -16)),
            lax.ppermute(v, "gz", route(device_count, 16)),
            lax.ppermute(u[2:3], "gz", route(device_count, 16)),
        ]
        shapes.append(jax.ShapeDtypeStruct((2, 6, count, wide), BF16))
    shapes.append(jax.ShapeDtypeStruct((3, 2 * count, 3 * (tiles - 2) * LANES), BF16))
    results = pl.pallas_call(
        functools.partial(interior_kernel, side, z_blocks),
        out_shape=shapes,
        in_specs=[vmem] * len(operands),
        out_specs=[vmem] * len(shapes),
        scratch_shapes=[pltpu.VMEM((4, 6, 16, wide), F32)],
        compiler_params=params,
        name="interior",
    )(*operands)
    vp, tab, coef, inner = results[0], results[1], results[2], results[-1]
    vz = list(results[3:-1])
    half = count // 2
    per = count // device_count
    lead = (device_count // 2, per, count)

    def products(start, stop, extra):
        with_border = len(extra) > 1
        operands = [directions, vp, tab, inner, *extra]
        shapes = [
            jax.ShapeDtypeStruct((stop - start, 2) + lead, F32),
            jax.ShapeDtypeStruct((stop - start, 2) + lead, BF16),
        ]
        scratch = [
            pltpu.VMEM((2 * count, 3 * wide), BF16),
            pltpu.VMEM((2, device_count // 2, 2, per, count), F32),
        ]
        if with_border:
            shapes.append(jax.ShapeDtypeStruct((3, 2 * count, 6 * LANES), BF16))
            scratch += [
                pltpu.VMEM((6, count, LANES), BF16),
                pltpu.VMEM((2 * 27, 8, LANES), F32),
            ]
        results = pl.pallas_call(
            functools.partial(products_kernel, side, sites, z_blocks, factor, start, stop, with_border),
            out_shape=shapes,
            in_specs=[smem] + [vmem] * (len(operands) - 1),
            out_specs=[vmem] * len(shapes),
            scratch_shapes=scratch,
            compiler_params=params,
            name=f"products_{start}",
        )(*operands)
        flat = (stop - start, 2, half, count)
        return results[0].reshape(flat), results[1].reshape(flat), results[2:]

    order = [2**n for n in range(device_count.bit_length() - 1)]
    other = [order[0], order[2], order[1]] + order[3:]
    cut = np_ // 2
    keep, send, (outer,) = products(0, cut, [coef, near, *halos, *vz])
    first = halve(keep, send, order, me)
    keep, send, _ = products(cut, np_, [outer])
    second = halve(keep, send, other, me)
    return jnp.concatenate([first, second], 0)


def solution(mesh):
    return jax.shard_map(
        body,
        mesh=mesh,
        in_specs=(
            P(("slab", "gz"), None, None, None, None),
            P(("slab", "gz"), None, None, None, None, None),
            P(),
            P(),
        ),
        out_specs=P("slab", None, "gz", None),
        check_vma=False,
    )
```

time: 241 us -> 74.2 us (0.31)
  local copies, waits for them, and re-layouts: 60.4 us -> 4.32 us
  waiting for transfers between devices: 72.5 us -> 16.8 us
  other arithmetic: 55.4 us -> 3.34 us
  Pallas kernels: 0 us -> 37.9 us
  between operations: 30.6 us -> 0.23 us
  matrix products: 9.04 us -> 0 us
    reduce_scatter x1 -> x0, waiting for transfers between devices: 72.1 us -> none  [body(): lax.psum_scatter(jnp.stack(blocks, 1) * factor, 'gz', scatter_dimension=0...]
    convert_element_type x54 -> x6, local copies, waits for them, and re-layouts: 48.6 us -> 0.17 us  [halve(): send = lax.dynamic_index_in_dim(split, 1 - mine, 3, False).astype(BF16)]
    pallas_call x0 -> x4, Pallas kernels: none -> 37.9 us  [the longest x2 30.3 us: products(): pl.pallas_call(functools.partial(products_kernel, side, sites, z_blocks,...]
    ppermute x8 -> x12, waiting for transfers between devices: 0.43 us -> 16.8 us  [the longest x8 16.8 us: halve(): got = lax.ppermute(send, 'gz', [(i, i ^ bit) for i in range(count)])]
    another operation x19 -> x0, other arithmetic: 15.9 us -> none
    sin x8 -> x0, other arithmetic: 15.3 us -> none  [body(): sin_part = jnp.sin(phase_angle)[None, None, :]]
    slice x8 -> x0, local copies, waits for them, and re-layouts: 9.45 us -> none  [the longest x2 3.44 us: body(): lax.slice_in_dim(grid_v, 1, length, 1, axis)]
    dot_general x8 -> x0, matrix products: 9.04 us -> none  [body(): lax.dot_general(left_side, right_side, (((0, 1, 3), (1, 2, 4)), ((), ()))...]
  transfers between devices with their start and end apart: 9 -> 12, of which waited for: 2 -> 6; matrix products, arithmetic and copies ran while one was open for 45% -> 5% of each run, Pallas kernels for 0% -> 27%
where the time goes in v2:
time: 74.2 us; the launch traced here: 73.8 us
  Pallas kernels  37.9 us (51%)
  waiting for transfers between devices  16.8 us (23%)
  starting transfers between devices  11.2 us (15%)
  local copies, waits for them, and re-layouts  4.32 us (6%)
  other arithmetic  3.34 us (5%)
    pallas_call x2, Pallas kernels, products(): pl.pallas_call(functools.partial(products_kernel, side, sites, z_blocks,...  30.3 us
    ppermute x8, waiting for transfers between devices, halve(): got = lax.ppermute(send, 'gz', [(i, i ^ bit) for i in range(count)])  16.8 us
    pallas_call x1, Pallas kernels, body(): pl.pallas_call(functools.partial(interior_kernel, side, z_blocks), out_sh...  7.23 us
    ppermute x4, starting transfers between devices, sent(): return lax.ppermute(face, 'gz', [(i, of(i)) for i in range(device_count)])  6.88 us
    ppermute x8, starting transfers between devices, halve(): got = lax.ppermute(send, 'gz', [(i, i ^ bit) for i in range(count)])  4.33 us
    unnamed x11, local copies, waits for them, and re-layouts  4.02 us
    add x8, other arithmetic, halve(): total = keep + got.astype(F32)  2.62 us
  transfers between devices with their start and end apart: 12, of which 6 were waited for; matrix products, arithmetic and copies ran while one was open for 5% of the time, Pallas kernels for 27%

profile of v2, /device:TPU:0, one launch (start us, length us, event | category | flops | bytes accessed | tf_op | source)
XLA Modules:
  0.0 73.8 jit_solution(2181362362913463543)
XLA Ops:
  0.0 1.5 %copy-done = bf16[1,2,3,256,576]{3,4,2,1,0:T(8,128)(2,1)S(1)} copy-done((bf16[1,2,3,256,576]{3,4,2,1,0:T(8,128)(2,1)S(1)}, bf16[1,2,3,256,576]{3,4,2,1,0:T(8,128)(2,1)}, u32[]{:S(2)}) %copy-start) | copy-done | bytes 1769496
  1.5 0.9 %copy-done.2 = bf16[1,3,2,3,3,576]{5,2,4,3,1,0:T(2,128)(2,1)S(1)} copy-done((bf16[1,3,2,3,3,576]{5,2,4,3,1,0:T(2,128)(2,1)S(1)}, bf16[1,3,2,3,3,576]{5,2,4,3,1,0:T(2,128)(2,1)}, u32[]{:S(2)}) %copy-start.2) | copy-done | bytes 62232
  2.7 0.5 collective-permute-start.3
  3.3 2.6 %collective-permute-start.1 = (bf16[176,256]{1,0:T(8,128)(2,1)S(1)}, bf16[176,256]{1,0:T(8,128)(2,1)S(1)}, u32[]{:S(2)}, u32[]{:S(2)}) collective-permute-start(bf16[176,256]{1,0:T(8,128)(2,1)S(1)} %get-tuple-element.27), channel_id=1, source_target_pairs={{0,4},{1,5},{2,6},{3,7},{4,8},{5,9},{6,10},{7,11},{8,12},{9,13},{1... | collective-permute-start | bytes 270344 | tf_op jit(solution)/shard_map/ppermute | solution.py:412
  5.9 1.4 %collective-permute-start.2 = (bf16[144,256]{1,0:T(8,128)(2,1)S(1)}, bf16[144,256]{1,0:T(8,128)(2,1)S(1)}, u32[]{:S(2)}, u32[]{:S(2)}) collective-permute-start(bf16[144,256]{1,0:T(8,128)(2,1)S(1)} %get-tuple-element.19.low_y), channel_id=1, source_target_pairs={{0,3},{1,0},{2,1},{3,2},{4,7},{5,4},{6,5},{7,6},{8,11},{9,8},{10,9... | collective-permute-start | bytes 221192 | tf_op jit(solution)/shard_map/ppermute | solution.py:412
  7.3 2.3 %collective-permute-start = (bf16[144,256]{1,0:T(8,128)(2,1)S(1)}, bf16[144,256]{1,0:T(8,128)(2,1)S(1)}, u32[]{:S(2)}, u32[]{:S(2)}) collective-permute-start(bf16[144,256]{1,0:T(8,128)(2,1)S(1)} %get-tuple-element.26), channel_id=1, source_target_pairs={{0,12},{1,13},{2,14},{3,15},{4,0},{5,1},{6,2},{7,3},{8,4},{9,5},{1... | collective-permute-start | bytes 221192 | tf_op jit(solution)/shard_map/ppermute | solution.py:412
  9.6 0.8 %copy.8.momenta_ref = s32[8,3]{1,0:T(8,128)S(1)} copy(s32[8,3]{0,1:T(4,128)} %param.6) | data formatting | bytes 192 | tf_op args[2]
  10.4 0.9 %copy-done.3 = bf16[1,3,2,3,3,576]{5,2,4,3,1,0:T(2,128)(2,1)S(1)} copy-done((bf16[1,3,2,3,3,576]{5,2,4,3,1,0:T(2,128)(2,1)S(1)}, bf16[1,3,2,3,3,576]{5,2,4,3,1,0:T(2,128)(2,1)}, u32[]{:S(2)}) %copy-start.3) | copy-done | bytes 62232
  11.3 7.2 %interior.1 = (bf16[6,256,640]{2,1,0:T(8,128)(2,1)S(1)}, f32[2,8,640]{2,1,0:T(8,128)S(1)}, f32[135,8,640]{2,1,0:T(8,128)S(1)}, bf16[3,512,1152]{2,1,0:T(8,128)(2,1)S(1)}) custom-call(s32[8,3]{1,0:T(8,128)S(1)} %copy.8.momenta_ref, bf16[2,3,576,256]{3,2,1,0:T(8,128)(2,1)S(1)} %bitcast.51, bf16[3,3,3,2,576]{4,3,2,1,0:T(2,128)(2,1)S(1)} %bitcast.53, ...), custom_call_target="tpu_custom_call" | custom-call | tf_op jit(solution)/shard_map/interior/pallas_call | solution.py:436
  18.5 17.3 %products_0.1 = (f32[4,2,8,16,256]{4,3,2,1,0:T(8,128)S(1)}, bf16[4,2,8,16,256]{4,3,2,1,0:T(8,128)(2,1)S(1)}, bf16[3,512,768]{2,1,0:T(8,128)(2,1)S(1)}) custom-call(s32[8]{0:T(128)S(1)} %copy-done.4, bf16[6,256,640]{2,1,0:T(8,128)(2,1)S(1)} %get-tuple-element.21.vp, f32[2,8,640]{2,1,0:T(8,128)S(1)} %get-tuple-element.22.tab, ...), custom_call_target="tpu_custom_call" | custom-call | tf_op jit(solution)/shard_map/products_0/pallas_call | solution.py:468
  35.9 13.0 %products_4.1 = (f32[4,2,8,16,256]{4,3,2,1,0:T(8,128)S(1)}, bf16[4,2,8,16,256]{4,3,2,1,0:T(8,128)(2,1)S(1)}) custom-call(s32[8]{0:T(128)S(1)} %copy-done.4, bf16[6,256,640]{2,1,0:T(8,128)(2,1)S(1)} %get-tuple-element.21.vp, f32[2,8,640]{2,1,0:T(8,128)S(1)} %get-tuple-element.22.tab, bf16[3,512,1152]{2,1,0:T(8,128)(2,1)S(1)} %get-tuple-element.23.inner_ref, ...), custom_call_target="tpu_custom_call" | custom-call | tf_op jit(solution)/shard_map/products_4/pallas_call | solution.py:468
  48.9 0.6 collective-permute-start.8
  49.5 1.2 %bitcast_add_fusion.1 = f32[4,2,128,256]{3,2,1,0:T(8,128)S(1)} fusion(f32[4,2,8,16,256]{4,3,2,1,0:T(8,128)S(1)} %get-tuple-element.28, bf16[4,2,128,256]{3,2,1,0:T(8,128)(2,1)} %collective-permute-done.4), kind=kLoop, calls=%fused_computation.1 | loop fusion | flops 524288 | bytes 2621440 | tf_op jit(solution)/shard_map/add | solution.py:359
  50.8 1.6 %collective-permute-start.5 = (bf16[4,2,64,256]{3,2,1,0:T(8,128)(2,1)S(1)}, bf16[4,2,64,256]{3,2,1,0:T(8,128)(2,1)S(1)}, u32[]{:S(2)}, u32[]{:S(2)}) collective-permute-start(bf16[4,2,64,256]{3,2,1,0:T(8,128)(2,1)S(1)} %bitcast.69), channel_id=1, source_target_pairs={{0,2},{1,3},{2,0},{3,1},{4,6},{5,7},{6,4},{7,5},{8,10},{9,11},{10,... | collective-permute-start | bytes 786440 | tf_op jit(solution)/shard_map/ppermute | solution.py:358
  52.3 1.2 %bitcast_add_fusion = f32[4,2,128,256]{3,2,1,0:T(8,128)S(1)} fusion(f32[4,2,8,16,256]{4,3,2,1,0:T(8,128)S(1)} %get-tuple-element.31, bf16[4,2,128,256]{3,2,1,0:T(8,128)(2,1)} %collective-permute-done.8), kind=kLoop, calls=%fused_computation | loop fusion | flops 524288 | bytes 2621440 | tf_op jit(solution)/shard_map/add | solution.py:359
  53.8 5.4 %collective-permute-done.5 = bf16[4,2,64,256]{3,2,1,0:T(8,128)(2,1)S(1)} collective-permute-done((bf16[4,2,64,256]{3,2,1,0:T(8,128)(2,1)S(1)}, bf16[4,2,64,256]{3,2,1,0:T(8,128)(2,1)S(1)}, u32[]{:S(2)}, u32[]{:S(2)}) %collective-permute-start.5) | collective-permute-done | bytes 262176 | tf_op jit(solution)/shard_map/ppermute | solution.py:358
  59.4 2.8 %collective-permute-done.9 = bf16[4,2,64,256]{3,2,1,0:T(8,128)(2,1)S(1)} collective-permute-done((bf16[4,2,64,256]{3,2,1,0:T(8,128)(2,1)S(1)}, bf16[4,2,64,256]{3,2,1,0:T(8,128)(2,1)S(1)}, u32[]{:S(2)}, u32[]{:S(2)}) %collective-permute-start.9) | collective-permute-done | bytes 262176 | tf_op jit(solution)/shard_map/ppermute | solution.py:358
  62.8 1.8 %collective-permute-done.6 = bf16[4,2,32,256]{3,2,1,0:T(8,128)(2,1)S(1)} collective-permute-done((bf16[4,2,32,256]{3,2,1,0:T(8,128)(2,1)S(1)}, bf16[4,2,32,256]{3,2,1,0:T(8,128)(2,1)S(1)}, u32[]{:S(2)}, u32[]{:S(2)}) %collective-permute-start.6) | collective-permute-done | bytes 131104 | tf_op jit(solution)/shard_map/ppermute | solution.py:358
  64.6 0.8 %collective-permute-start.7 = (bf16[4,2,16,256]{3,2,1,0:T(8,128)(2,1)S(1)}, bf16[4,2,16,256]{3,2,1,0:T(8,128)(2,1)S(1)}, u32[]{:S(2)}, u32[]{:S(2)}) collective-permute-start(bf16[4,2,16,256]{3,2,1,0:T(8,128)(2,1)S(1)} %fusion), channel_id=1, source_target_pairs={{0,8},{1,9},{2,10},{3,11},{4,12},{5,13},{6,14},{7,15},{8,0},{9,1},... | collective-permute-start | bytes 196616 | tf_op jit(solution)/shard_map/ppermute | solution.py:358
  65.4 2.0 %collective-permute-done.10 = bf16[4,2,32,256]{3,2,1,0:T(8,128)(2,1)S(1)} collective-permute-done((bf16[4,2,32,256]{3,2,1,0:T(8,128)(2,1)S(1)}, bf16[4,2,32,256]{3,2,1,0:T(8,128)(2,1)S(1)}, u32[]{:S(2)}, u32[]{:S(2)}) %collective-permute-start.10) | collective-permute-done | bytes 131104 | tf_op jit(solution)/shard_map/ppermute | solution.py:358
  67.4 0.8 %collective-permute-start.11 = (bf16[4,2,16,256]{3,2,1,0:T(8,128)(2,1)S(1)}, bf16[4,2,16,256]{3,2,1,0:T(8,128)(2,1)S(1)}, u32[]{:S(2)}, u32[]{:S(2)}) collective-permute-start(bf16[4,2,16,256]{3,2,1,0:T(8,128)(2,1)S(1)} %fusion.1), channel_id=1, source_target_pairs={{0,8},{1,9},{2,10},{3,11},{4,12},{5,13},{6,14},{7,15},{8,0},{9,1},... | collective-permute-start | bytes 196616 | tf_op jit(solution)/shard_map/ppermute | solution.py:358
  68.2 3.1 %collective-permute-done.7 = bf16[4,2,16,256]{3,2,1,0:T(8,128)(2,1)S(1)} collective-permute-done((bf16[4,2,16,256]{3,2,1,0:T(8,128)(2,1)S(1)}, bf16[4,2,16,256]{3,2,1,0:T(8,128)(2,1)S(1)}, u32[]{:S(2)}, u32[]{:S(2)}) %collective-permute-start.7) | collective-permute-done | bytes 65568 | tf_op jit(solution)/shard_map/ppermute | solution.py:358
  71.3 1.8 %collective-permute-done.11 = bf16[4,2,16,256]{3,2,1,0:T(8,128)(2,1)S(1)} collective-permute-done((bf16[4,2,16,256]{3,2,1,0:T(8,128)(2,1)S(1)}, bf16[4,2,16,256]{3,2,1,0:T(8,128)(2,1)S(1)}, u32[]{:S(2)}, u32[]{:S(2)}) %collective-permute-start.11) | collective-permute-done | bytes 65568 | tf_op jit(solution)/shard_map/ppermute | solution.py:358
  73.1 0.7 pad_maximum_fusion
  (34 shorter events, 1.5 us)
Async XLA Ops:
  0.0 18.5 %copy-start.4 = (s32[8]{0:T(128)S(1)}, s32[8]{0:T(128)}, u32[]{:S(2)}) copy-start(s32[8]{0:T(128)} %directions_ref.3) | copy-start | bytes 100
  0.0 1.5 %copy-start = (bf16[1,2,3,256,576]{3,4,2,1,0:T(8,128)(2,1)S(1)}, bf16[1,2,3,256,576]{3,4,2,1,0:T(8,128)(2,1)}, u32[]{:S(2)}) copy-start(bf16[1,2,3,256,576]{3,4,2,1,0:T(8,128)(2,1)} %param.4) | copy-start | bytes 5308420
  1.5 0.9 %copy-start.2 = (bf16[1,3,2,3,3,576]{5,2,4,3,1,0:T(2,128)(2,1)S(1)}, bf16[1,3,2,3,3,576]{5,2,4,3,1,0:T(2,128)(2,1)}, u32[]{:S(2)}) copy-start(bf16[1,3,2,3,3,576]{5,2,4,3,1,0:T(2,128)(2,1)} %param.5) | copy-start | bytes 186628
  2.4 8.0 %copy-start.1 = (bf16[1,2,3,256,576]{3,4,2,1,0:T(8,128)(2,1)S(1)}, bf16[1,2,3,256,576]{3,4,2,1,0:T(8,128)(2,1)}, u32[]{:S(2)}) copy-start(bf16[1,2,3,256,576]{3,4,2,1,0:T(8,128)(2,1)} %param.4) | copy-start | bytes 5308420
  2.7 15.8 %collective-permute-start.3 = (bf16[176,256]{1,0:T(8,128)(2,1)S(1)}, bf16[176,256]{1,0:T(8,128)(2,1)S(1)}, u32[]{:S(2)}, u32[]{:S(2)}) collective-permute-start(bf16[176,256]{1,0:T(8,128)(2,1)S(1)} %get-tuple-element.20.high_y), channel_id=1, source_target_pairs={{0,1},{1,2},{2,3},{3,0},{4,5},{5,6},{6,7},{7,4},{8,9},{9,10},{10,1... | collective-permute-start | bytes 270344 | tf_op jit(solution)/shard_map/ppermute | solution.py:412
  3.3 15.2 %collective-permute-start.1 = (bf16[176,256]{1,0:T(8,128)(2,1)S(1)}, bf16[176,256]{1,0:T(8,128)(2,1)S(1)}, u32[]{:S(2)}, u32[]{:S(2)}) collective-permute-start(bf16[176,256]{1,0:T(8,128)(2,1)S(1)} %get-tuple-element.27), channel_id=1, source_target_pairs={{0,4},{1,5},{2,6},{3,7},{4,8},{5,9},{6,10},{7,11},{8,12},{9,13},{1... | collective-permute-start | bytes 270344 | tf_op jit(solution)/shard_map/ppermute | solution.py:412
  5.9 12.6 %collective-permute-start.2 = (bf16[144,256]{1,0:T(8,128)(2,1)S(1)}, bf16[144,256]{1,0:T(8,128)(2,1)S(1)}, u32[]{:S(2)}, u32[]{:S(2)}) collective-permute-start(bf16[144,256]{1,0:T(8,128)(2,1)S(1)} %get-tuple-element.19.low_y), channel_id=1, source_target_pairs={{0,3},{1,0},{2,1},{3,2},{4,7},{5,4},{6,5},{7,6},{8,11},{9,8},{10,9... | collective-permute-start | bytes 221192 | tf_op jit(solution)/shard_map/ppermute | solution.py:412
  7.3 11.2 %collective-permute-start = (bf16[144,256]{1,0:T(8,128)(2,1)S(1)}, bf16[144,256]{1,0:T(8,128)(2,1)S(1)}, u32[]{:S(2)}, u32[]{:S(2)}) collective-permute-start(bf16[144,256]{1,0:T(8,128)(2,1)S(1)} %get-tuple-element.26), channel_id=1, source_target_pairs={{0,12},{1,13},{2,14},{3,15},{4,0},{5,1},{6,2},{7,3},{8,4},{9,5},{1... | collective-permute-start | bytes 221192 | tf_op jit(solution)/shard_map/ppermute | solution.py:412
  10.4 0.9 %copy-start.3 = (bf16[1,3,2,3,3,576]{5,2,4,3,1,0:T(2,128)(2,1)S(1)}, bf16[1,3,2,3,3,576]{5,2,4,3,1,0:T(2,128)(2,1)}, u32[]{:S(2)}) copy-start(bf16[1,3,2,3,3,576]{5,2,4,3,1,0:T(2,128)(2,1)} %param.5) | copy-start | bytes 186628
  35.8 13.7 %collective-permute-start.4 = (bf16[4,2,128,256]{3,2,1,0:T(8,128)(2,1)S(1)}, bf16[4,2,128,256]{3,2,1,0:T(8,128)(2,1)}, u32[]{:S(2)}, u32[]{:S(2)}) collective-permute-start(bf16[4,2,128,256]{3,2,1,0:T(8,128)(2,1)S(1)} %bitcast.54), channel_id=1, source_target_pairs={{0,1},{1,0},{2,3},{3,2},{4,5},{5,4},{6,7},{7,6},{8,9},{9,8},{10,11... | collective-permute-start | bytes 1572872 | tf_op jit(solution)/shard_map/ppermute | solution.py:358
  48.9 3.4 %collective-permute-start.8 = (bf16[4,2,128,256]{3,2,1,0:T(8,128)(2,1)S(1)}, bf16[4,2,128,256]{3,2,1,0:T(8,128)(2,1)}, u32[]{:S(2)}, u32[]{:S(2)}) collective-permute-start(bf16[4,2,128,256]{3,2,1,0:T(8,128)(2,1)S(1)} %bitcast.55), channel_id=1, source_target_pairs={{0,1},{1,0},{2,3},{3,2},{4,5},{5,4},{6,7},{7,6},{8,9},{9,8},{10,11... | collective-permute-start | bytes 1572872 | tf_op jit(solution)/shard_map/ppermute | solution.py:358
  50.8 8.4 %collective-permute-start.5 = (bf16[4,2,64,256]{3,2,1,0:T(8,128)(2,1)S(1)}, bf16[4,2,64,256]{3,2,1,0:T(8,128)(2,1)S(1)}, u32[]{:S(2)}, u32[]{:S(2)}) collective-permute-start(bf16[4,2,64,256]{3,2,1,0:T(8,128)(2,1)S(1)} %bitcast.69), channel_id=1, source_target_pairs={{0,2},{1,3},{2,0},{3,1},{4,6},{5,7},{6,4},{7,5},{8,10},{9,11},{10,... | collective-permute-start | bytes 786440 | tf_op jit(solution)/shard_map/ppermute | solution.py:358
  53.6 8.6 %collective-permute-start.9 = (bf16[4,2,64,256]{3,2,1,0:T(8,128)(2,1)S(1)}, bf16[4,2,64,256]{3,2,1,0:T(8,128)(2,1)S(1)}, u32[]{:S(2)}, u32[]{:S(2)}) collective-permute-start(bf16[4,2,64,256]{3,2,1,0:T(8,128)(2,1)S(1)} %bitcast.68), channel_id=1, source_target_pairs={{0,4},{1,5},{2,6},{3,7},{4,0},{5,1},{6,2},{7,3},{8,12},{9,13},{10,... | collective-permute-start | bytes 786440 | tf_op jit(solution)/shard_map/ppermute | solution.py:358
  59.3 5.2 %collective-permute-start.6 = (bf16[4,2,32,256]{3,2,1,0:T(8,128)(2,1)S(1)}, bf16[4,2,32,256]{3,2,1,0:T(8,128)(2,1)S(1)}, u32[]{:S(2)}, u32[]{:S(2)}) collective-permute-start(bf16[4,2,32,256]{3,2,1,0:T(8,128)(2,1)S(1)} %bitcast.70), channel_id=1, source_target_pairs={{0,4},{1,5},{2,6},{3,7},{4,0},{5,1},{6,2},{7,3},{8,12},{9,13},{10,... | collective-permute-start | bytes 393224 | tf_op jit(solution)/shard_map/ppermute | solution.py:358
  62.3 5.0 %collective-permute-start.10 = (bf16[4,2,32,256]{3,2,1,0:T(8,128)(2,1)S(1)}, bf16[4,2,32,256]{3,2,1,0:T(8,128)(2,1)S(1)}, u32[]{:S(2)}, u32[]{:S(2)}) collective-permute-start(bf16[4,2,32,256]{3,2,1,0:T(8,128)(2,1)S(1)} %bitcast.71), channel_id=1, source_target_pairs={{0,2},{1,3},{2,0},{3,1},{4,6},{5,7},{6,4},{7,5},{8,10},{9,11},{10,... | collective-permute-start | bytes 393224 | tf_op jit(solution)/shard_map/ppermute | solution.py:358
  64.6 6.7 %collective-permute-start.7 = (bf16[4,2,16,256]{3,2,1,0:T(8,128)(2,1)S(1)}, bf16[4,2,16,256]{3,2,1,0:T(8,128)(2,1)S(1)}, u32[]{:S(2)}, u32[]{:S(2)}) collective-permute-start(bf16[4,2,16,256]{3,2,1,0:T(8,128)(2,1)S(1)} %fusion), channel_id=1, source_target_pairs={{0,8},{1,9},{2,10},{3,11},{4,12},{5,13},{6,14},{7,15},{8,0},{9,1},... | collective-permute-start | bytes 196616 | tf_op jit(solution)/shard_map/ppermute | solution.py:358
  67.4 5.7 %collective-permute-start.11 = (bf16[4,2,16,256]{3,2,1,0:T(8,128)(2,1)S(1)}, bf16[4,2,16,256]{3,2,1,0:T(8,128)(2,1)S(1)}, u32[]{:S(2)}, u32[]{:S(2)}) collective-permute-start(bf16[4,2,16,256]{3,2,1,0:T(8,128)(2,1)S(1)} %fusion.1), channel_id=1, source_target_pairs={{0,8},{1,9},{2,10},{3,11},{4,12},{5,13},{6,14},{7,15},{8,0},{9,1},... | collective-permute-start | bytes 196616 | tf_op jit(solution)/shard_map/ppermute | solution.py:358
